TPU v7x, 32 devices: a whole 2x2x4 slice. The times are simulated.
32 devices in a mesh: groups: 2 (over y), expert: 4 (over z), tensor: 2 (over x), inner: 2 (over core).
Axes of the slice: x: 2, y: 2, z: 4, core: 2. Of those that a mesh axis runs over, the one named last changes fastest.
Arguments:
- tokens: bfloat16 [1024, 7168], P(('groups', 'expert'), ('tensor', 'inner')), parts along dimension 0, may hold values from -6 to 6
- expert_ids: int32 [1024, 8], P(('groups', 'expert')), parts along dimension 0, may hold values from 0 to 31, all different within a row; in each aligned block of 128 rows (0 to 127, 128 to 255, ...) at most 96 rows name the same one
- gate_weights: float32 [1024, 8], P(('groups', 'expert')), parts along dimension 0, may hold values from 0.05 to 0.45
- base_weights: bfloat16 [3, 1024, 7168], P(None, 'expert', ('tensor', 'inner')), may hold values from -0.0625 to 0.0625
- in_factor: bfloat16 [3840, 7168], P('expert', ('tensor', 'inner')), may hold values from -0.0625 to 0.0625
- out_factors: bfloat16 [2, 3840, 1024], P(None, 'expert', ('tensor', 'inner')), may hold values from -0.375 to 0.375
- ranks: int32 [32], P('expert'), may hold values from 64 to 512, as said below
Outputs:
- mixed: bfloat16 [1024, 7168], P(('groups', 'expert'), ('tensor', 'inner')), parts along dimension 0
There are 2 independent parts, one for each index of `groups`. A program takes and returns all parts, laid end to end along the dimension named above; an argument that names none is the same for every part. Nothing has to cross between parts.
Inputs may be any that keep to these rules, and one draw needn't show every extreme that they name: `expert_ids`: in each aligned block of 128 tokens no expert is chosen more than 96 times, and some expert is chosen exactly 96 times; the experts of one token differ. The ranks of each aligned block of 8 experts sum to exactly 960.
All inputs are finite; a program needn't handle non-finite values.
Results may differ from a plain program's by a relative error of at most 0.023.
Values may be sent and summed in bfloat16 or wider, within the bound.
No kernel may reach another device: no remote copies, remote signals or barrier semaphores. Data moves between devices by JAX's collectives and lax.ppermute only.
A program may use at most 64 MiB of HBM per device.

v0:
```python
import jax
import jax.numpy as jnp
from jax import lax
from jax.sharding import PartitionSpec as P

RANK_MAX = 512


def on_device(tokens, expert_ids, gate_weights, base_weights, in_factor, out_factors, ranks):
    tok_rows, feat_slice = tokens.shape
    top_count = expert_ids.shape[1]
    owners = lax.axis_size("expert")
    local_count = ranks.shape[0]
    experts = local_count * owners
    capacity = min(tok_rows, 3 * tok_rows * top_count // experts)
    hidden_slice = out_factors.shape[2]
    width = RANK_MAX
    gathered = lax.all_gather(base_weights, "expert", axis=1, tiled=True)
    partial_value = jnp.einsum(
        "td,gfd->tgf", tokens, gathered[:2], preferred_element_type=jnp.float32
    )
    base_rows = lax.psum_scatter(
        partial_value.astype(jnp.bfloat16), ("tensor", "inner"), scatter_dimension=2, tiled=True
    )
    pairs = tok_rows * top_count
    flat_ids = expert_ids.reshape(pairs)
    columns = lax.broadcasted_iota(jnp.int32, (pairs, experts), 1)
    onehot = (flat_ids[:, None] == columns).astype(jnp.bfloat16)
    row_pos = lax.broadcasted_iota(jnp.int32, (pairs, pairs), 0)
    col_pos = lax.broadcasted_iota(jnp.int32, (pairs, pairs), 1)
    earlier = (row_pos > col_pos).astype(jnp.bfloat16)
    counts = jnp.dot(earlier, onehot, preferred_element_type=jnp.float32)
    slot = jnp.sum(counts * onehot.astype(jnp.float32), axis=1).astype(jnp.int32)
    owner_of = flat_ids // local_count
    member_of = flat_ids % local_count
    target = (member_of * owners + owner_of) * capacity + slot
    source_row = lax.broadcasted_iota(jnp.int32, (pairs,), 0) // top_count
    outgoing = jnp.zeros((local_count * owners * capacity, feat_slice), jnp.bfloat16)
    outgoing = outgoing.at[target].set(tokens[source_row])
    outgoing = outgoing.reshape(local_count, owners, capacity, feat_slice)
    arrived = lax.all_to_all(outgoing, "expert", split_axis=1, concat_axis=1, tiled=True)
    slots = owners * capacity
    arrived = arrived.reshape(local_count, slots, feat_slice)
    starts = jnp.cumsum(ranks) - ranks
    in_pad = jnp.concatenate([in_factor, jnp.zeros((width, feat_slice), jnp.bfloat16)], 0)
    out_pad = jnp.concatenate([out_factors, jnp.zeros((2, width, hidden_slice), jnp.bfloat16)], 1)
    within = lax.broadcasted_iota(jnp.int32, (1, width), 1)
    terms = []
    for member in range(local_count):
        window = lax.dynamic_slice_in_dim(in_pad, starts[member], width, 0)
        terms.append(
            lax.dot_general(
                arrived[member],
                window,
                (((1,), (1,)), ((), ())),
                preferred_element_type=jnp.float32,
            )
        )
    stacked = jnp.stack(
        [
            jnp.where(within < ranks[member], terms[member], jnp.float32(0.0))
            for member in range(local_count)
        ]
    )
    summed = lax.psum(stacked.astype(jnp.bfloat16), ("tensor", "inner"))
    latents = [summed[member] for member in range(local_count)]
    outputs = []
    for member in range(local_count):
        factor = lax.dynamic_slice_in_dim(out_pad, starts[member], width, 1)
        outputs.append(
            jnp.einsum(
                "rc,gcf->rgf", latents[member], factor, preferred_element_type=jnp.float32
            ).astype(jnp.bfloat16)
        )
    replies = jnp.stack(outputs).reshape(local_count, owners, capacity, 2, hidden_slice)
    returned = lax.all_to_all(replies, "expert", split_axis=1, concat_axis=1, tiled=True)
    returned = returned.reshape(local_count * owners * capacity, 2, hidden_slice)
    delta = returned[target].reshape(tok_rows, top_count, 2, hidden_slice)
    summed_rows = base_rows.astype(jnp.float32)[:, None] + delta.astype(jnp.float32)
    hidden = (jax.nn.silu(summed_rows[:, :, 0]) * summed_rows[:, :, 1]).astype(jnp.bfloat16)
    combined = jnp.sum(gate_weights[:, :, None] * hidden.astype(jnp.float32), axis=1).astype(
        jnp.bfloat16
    )
    full_hidden = lax.all_gather(combined, ("tensor", "inner"), axis=1, tiled=True)
    return jnp.dot(full_hidden, gathered[2], preferred_element_type=jnp.float32).astype(
        jnp.bfloat16
    )


def solution(mesh):
    return jax.shard_map(
        on_device,
        mesh=mesh,
        in_specs=(
            P(("groups", "expert"), ("tensor", "inner")),
            P(("groups", "expert"), None),
            P(("groups", "expert"), None),
            P(None, "expert", ("tensor", "inner")),
            P("expert", ("tensor", "inner")),
            P(None, "expert", ("tensor", "inner")),
            P("expert"),
        ),
        out_specs=P(("groups", "expert"), ("tensor", "inner")),
        check_vma=False,
    )
```

profile of v0, /device:TPU:0, one launch (start us, length us, event | category | flops | bytes accessed | tf_op | source)
XLA Modules:
  0.0 655.0 jit_solution(18073991329550731420)
XLA Ops:
  7.4 0.8 copy.40
  9.0 31.4 %scatter_custom_fusion = bf16[3072,1792]{1,0:T(8,128)(2,1)} fusion(s32[1024]{0:T(1024)S(1)} %bitcast.155, bf16[]{:T(256)} %constant.47.clone.1, bf16[128,1792]{1,0:T(8,128)(2,1)S(1)} %copy-done, s32[1024]{0:T(1024)S(1)} %broadcast_clamp_fusion.1), kind=kCustom, calls=%fused_computation.13 | custom fusion | bytes 11010050 | tf_op jit(solution)/shard_map/scatter | solution.py:39
  40.5 9.6 %copy.42 = bf16[8,4,96,1792]{3,2,0,1:T(8,128)(2,1)} copy(bf16[8,4,96,1792]{3,2,1,0:T(8,128)(2,1)} %bitcast.135) | data formatting | bytes 22020096 | tf_op jit(solution)/shard_map/reshape | solution.py:40
  50.1 6.5 all-to-all-start
  75.1 0.7 iota_compare_fusion.12
  76.3 0.7 iota_compare_fusion.10
  78.4 218.9 %all-to-all-done = bf16[8,4,96,1792]{3,2,0,1:T(8,128)(2,1)} async-done(((bf16[8,4,96,1792]{3,2,0,1:T(8,128)(2,1)}), bf16[8,4,96,1792]{3,2,0,1:T(8,128)(2,1)}, u32[]{:S(2)}, u32[]{:S(2)}) %all-to-all-start) | async-done | bytes 11010080 | tf_op jit(solution)/shard_map/all_to_all | solution.py:41
  297.3 4.9 fusion.91
  302.5 1.9 fusion.50
  304.4 1.9 fusion.48
  306.3 1.9 fusion.46
  308.2 1.9 fusion.44
  310.1 1.9 fusion.42
  312.0 1.9 fusion.40
  313.9 1.9 fusion.38
  315.7 1.9 fusion.36
  318.2 67.3 %all-reduce.4.cloned.1.call-done = bf16[8,384,512]{2,1,0:T(8,128)(2,1)} async-done(((bf16[8,384,512]{2,1,0:T(8,128)(2,1)}), bf16[8,384,512]{2,1,0:T(8,128)(2,1)}) %all-reduce.4.cloned.1.call-update) | async-done | bytes 3145744 | tf_op jit(solution)/shard_map/psum | solution.py:65
  385.5 1.6 convolution_convert_fusion.7
  387.2 1.5 convolution_convert_fusion.6
  392.1 1.9 copy.54
  394.0 4.7 all-to-all-start.1
  398.7 179.8 %all-gather.2.cloned.1.call-done = bf16[3,1024,1792]{2,1,0:T(8,128)(2,1)} async-done(((bf16[3,256,1792]{2,1,0:T(8,128)(2,1)}), bf16[3,1024,1792]{2,1,0:T(8,128)(2,1)}) %all-gather.2.cloned.1.call-update) | async-done | bytes 11010064 | tf_op jit(solution)/shard_map/all_gather | solution.py:18
  578.5 6.3 fusion.16
  585.0 19.8 %reduce-scatter.2.cloned.1.call-done = bf16[128,2,256]{2,0,1:T(8,128)(2,1)} async-done(((bf16[128,2,1024]{2,0,1:T(8,128)(2,1)}), bf16[128,2,256]{2,0,1:T(8,128)(2,1)}) %reduce-scatter.2.cloned.1.call-update) | async-done | bytes 131088 | tf_op jit(solution)/shard_map/reduce_scatter | solution.py:22
  604.8 1.0 copy.39
  605.9 2.2 copy.51
  608.0 20.6 %copy.52 = bf16[3072,2,256]{2,1,0:T(2,128)(2,1)} copy(bf16[3072,2,256]{2,0,1:T(8,128)(2,1)S(1)} %bitcast.136) | data formatting | bytes 6291456 | tf_op jit(solution)/shard_map/reshape | solution.py:77
  628.6 6.1 gather_fusion
  634.7 1.3 convert_add_fusion
  636.0 1.6 fusion.92
  638.2 5.8 all_gather.7
  643.9 3.5 fusion.7
  (52 shorter events, 10.9 us)
Async XLA Ops:
  7.4 1.7 copy-start
  50.1 6.5 copy-start.3
  50.1 247.2 %all-to-all-start = ((bf16[8,4,96,1792]{3,2,0,1:T(8,128)(2,1)}), bf16[8,4,96,1792]{3,2,0,1:T(8,128)(2,1)}, u32[]{:S(2)}, u32[]{:S(2)}) async-start(bf16[8,4,96,1792]{3,2,0,1:T(8,128)(2,1)} %copy.42), calls=%async_computation.1 | async-start | bytes 22020096 | tf_op jit(solution)/shard_map/all_to_all | solution.py:41
  56.6 329.0 %all-reduce.4.cloned.1.call-start = ((), (), s32[]{:S(2)}) async-start(), calls=%async_computation.5 | async-start | bytes 6291456 | tf_op jit(solution)/shard_map/psum | solution.py:65
  297.3 5.2 copy-start.5
  317.6 67.9 %copy-start.1 = (bf16[2,960,256]{2,1,0:T(8,128)(2,1)S(1)}, bf16[2,960,256]{2,1,0:T(8,128)(2,1)}, u32[]{:S(2)}) copy-start(bf16[2,960,256]{2,1,0:T(8,128)(2,1)} %param.12) | copy-start | bytes 2949124
  317.6 260.9 %all-gather.2.cloned.1.call-start = ((), (), s32[]{:S(2)}) async-start(), calls=%async_computation.3 | async-start | bytes 13762560 | tf_op jit(solution)/shard_map/all_gather | solution.py:18
  385.5 3.2 copy-start.2
  394.0 211.9 %all-to-all-start.1 = ((bf16[8,4,96,2,256]{4,2,0,3,1:T(8,128)(2,1)}), bf16[8,4,96,2,256]{4,2,0,3,1:T(8,128)(2,1)}, u32[]{:S(2)}, u32[]{:S(2)}) async-start(bf16[8,4,96,2,256]{4,2,0,3,1:T(8,128)(2,1)} %copy.54), calls=%async_computation.2 | async-start | bytes 6291456 | tf_op jit(solution)/shard_map/all_to_all | solution.py:76
  398.6 186.3 %copy-start.4 = (f32[128,8]{0,1:T(8,128)S(1)}, f32[128,8]{0,1:T(8,128)}, u32[]{:S(2)}) copy-start(f32[128,8]{0,1:T(8,128)} %param.9) | copy-start | bytes 12292
  398.7 206.2 %reduce-scatter.2.cloned.1.call-start = ((), (), s32[]{:S(2)}) async-start(), calls=%async_computation.4 | async-start | bytes 655360 | tf_op jit(solution)/shard_map/reduce_scatter | solution.py:22
Sparse Core Ops, SparseCore 0:
  317.8 67.7 all-reduce.3
  585.0 19.7 reduce-scatter.1
Sparse Core Ops, SparseCore 1:
  319.7 258.8 all-gather.1
where the time goes:
time: 664 us; the launch traced here: 655 us
  waiting for transfers between devices  486 us (73%)
  local copies, waits for them, and re-layouts  82.3 us (12%)
  matrix products  31.7 us (5%)
  between operations  30.5 us (5%)
  starting transfers between devices  11.4 us (2%)
  other arithmetic  7.15 us (1%)
    all_to_all x1, waiting for transfers between devices, on_device(): lax.all_to_all(outgoing, 'expert', split_axis=1, concat_axis=1, tiled=True)  219 us
    all_gather x1, waiting for transfers between devices, on_device(): gathered = lax.all_gather(base_weights, 'expert', axis=1, tiled=True)  180 us
    psum x1, waiting for transfers between devices, on_device(): summed = lax.psum(stacked.astype(jnp.bfloat16), ('tensor', 'inner'))  67.3 us
    scatter x1, local copies, waits for them, and re-layouts, on_device(): outgoing = outgoing.at[target].set(tokens[source_row])  31.4 us
    reshape x1, local copies, waits for them, and re-layouts, on_device(): returned.reshape(local_count * owners * capacity, 2, hidden_slice)  20.6 us
    reduce_scatter x1, waiting for transfers between devices, on_device(): lax.psum_scatter(partial_value.astype(jnp.bfloat16), ('tensor', 'inner'),...  19.8 us
    dot_general x8, matrix products, on_device(): lax.dot_general(arrived[member], window, (((1,), (1,)), ((), ())), prefer...  15.2 us
  transfers between devices with their start and end apart: 5, of which 4 were waited for; matrix products, arithmetic and copies ran while one was open for 3% of the time, Pallas kernels for 0%

commit v1 on v0

v1 whole, which is shorter than its diff:
```python
import jax
import jax.numpy as jnp
from jax import lax
from jax.sharding import PartitionSpec as P

BF = jnp.bfloat16
F32 = jnp.float32
LINE_MAX = 8


def dot(lhs, rhs, dims):
    return lax.dot_general(lhs, rhs, (dims, ((), ())), preferred_element_type=F32)


def chain_gather(value, axis, first=None):
    size = lax.axis_size(axis)
    if size > LINE_MAX:
        return lax.all_gather(value, axis, axis=0, tiled=True)
    up = [(j, j + 1) for j in range(size - 1)]
    down = [(j + 1, j) for j in range(size - 1)]
    left, right = [], []
    from_left, from_right = value, value
    for _ in range(size - 1):
        from_left = lax.ppermute(from_left, axis, up)
        from_right = lax.ppermute(from_right, axis, down)
        left.append(from_left)
        right.append(from_right)
    line = jnp.concatenate(left[::-1] + [value] + right, 0)
    rows = value.shape[0]
    return lax.dynamic_slice_in_dim(line, (size - 1 - lax.axis_index(axis)) * rows, size * rows, 0)


def direct_gather(value, axis):
    size = lax.axis_size(axis)
    if size == 1:
        return value
    if size > LINE_MAX:
        return lax.all_gather(value, axis, axis=0, tiled=True)
    got = [value]
    for shift in range(1, size):
        got.append(lax.ppermute(value, axis, [(j, (j + shift) % size) for j in range(size)]))
    rows = value.shape[0]
    line = jnp.concatenate(got[:0:-1] + [value] + got[:0:-1], 0)
    return lax.dynamic_slice_in_dim(line, (size - 1 - lax.axis_index(axis)) * rows, size * rows, 0)


def scatter_sum(piece_of, axis):
    size = lax.axis_size(axis)
    index = lax.axis_index(axis)
    got = []
    for shift in range(1, size):
        sent = piece_of((index + shift) % size).astype(BF)
        got.append(lax.ppermute(sent, axis, [(j, (j + shift) % size) for j in range(size)]))
    total = piece_of(index).astype(F32)
    for term in got:
        total = total + term.astype(F32)
    return total


def after(value, *others):
    return lax.optimization_barrier((value,) + others)[0]


def on_device(tokens, expert_ids, gate_weights, base_weights, in_factor, out_factors, ranks):
    rows, feats = tokens.shape
    owners = lax.axis_size("expert")
    tensors, inners = lax.axis_size("tensor"), lax.axis_size("inner")
    copies = lax.axis_size("groups")
    local = ranks.shape[0]
    experts = local * owners
    units = base_weights.shape[1]
    hidden_all = units * owners
    width = in_factor.shape[0]
    sub = rows // (tensors * inners)
    z = lax.axis_index("expert")
    core = lax.axis_index("inner")
    part = lax.axis_index("tensor") * inners + core

    gathered = chain_gather(tokens, "expert")

    own_ids = lax.dynamic_slice_in_dim(expert_ids, part * sub, sub, 0)
    own_gates = lax.dynamic_slice_in_dim(gate_weights, part * sub, sub, 0)
    columns = lax.broadcasted_iota(jnp.int32, (1, 1, experts), 2)
    dense = jnp.sum(jnp.where(own_ids[:, :, None] == columns, own_gates[:, :, None], 0.0), axis=1)
    dense = direct_gather(dense, "expert")
    gates = lax.dynamic_slice_in_dim(dense, z * local, local, 1)

    factors = direct_gather(direct_gather(out_factors[None], "tensor"), "inner")

    blocks = gathered.reshape(owners, tensors, inners, sub, feats)
    base_flat = base_weights[:2].reshape(2 * units, feats)

    def product(weights):
        def of_core(index):
            picked = lax.dynamic_index_in_dim(blocks, index, 2, keepdims=False)
            picked = picked.reshape(owners * tensors * sub, feats)
            return dot(picked, weights, ((1,), (1,)))

        halves = scatter_sum(of_core, "inner").reshape(owners, tensors, sub, weights.shape[0])

        def of_tensor(index):
            return lax.dynamic_index_in_dim(halves, index, 1, keepdims=False)

        return scatter_sum(of_tensor, "tensor").reshape(owners * sub, weights.shape[0]).astype(BF)

    base_rows = product(base_flat)
    latent = product(in_factor)

    base_all = chain_gather(base_rows.reshape(1, owners * sub, 2, units), "expert")

    down = base_weights[2]
    if owners <= LINE_MAX and units % copies == 0 and copies > 1:
        piece = units // copies
        g = lax.axis_index("groups")
        mine = lax.dynamic_slice_in_dim(down, g * piece, piece, 0)
        mine = after(mine, gathered)
        mine = chain_gather(mine[None], "expert")
        down_all = direct_gather(mine[None], "groups")
        down_all = jnp.moveaxis(down_all, 0, 1).reshape(hidden_all, feats)
    else:
        down_all = lax.all_gather(down, "expert", axis=0, tiled=True)

    ends = jnp.cumsum(ranks)
    position = lax.broadcasted_iota(jnp.int32, (1, width), 1)
    owner_of = jnp.sum((position[:, :, None] >= ends[None, None, :]).astype(jnp.int32), axis=2)
    member = lax.broadcasted_iota(jnp.int32, (local, 1, 1), 0)
    base_all = base_all.transpose(1, 2, 0, 3).reshape(owners * sub, 2, hidden_all)

    def mix(operands):
        latent_rows, base_part, gate_part = operands
        count = latent_rows.shape[0]
        spread = jnp.where(owner_of[None] == member, latent_rows[None], jnp.zeros((), BF))
        spread = spread.reshape(local * count, width)
        both = []
        for g in range(2):
            parts = []
            for block in range(tensors * inners):
                source = (block % inners) * tensors + block // inners
                parts.append(dot(spread, factors[source, g], ((1,), (0,))).astype(BF))
            delta = jnp.concatenate(parts, 1).reshape(local, count, hidden_all)
            both.append(base_part[None, :, g].astype(F32) + delta.astype(F32))
        hidden = (jax.nn.silu(both[0]) * both[1]).astype(BF).astype(F32)
        weight = gate_part.T[:, :, None]
        return jnp.sum(jnp.where(weight > 0, weight * hidden, 0.0), axis=0)

    chunks = max(1, owners * sub // rows)
    if chunks == 1:
        combined = mix((latent, base_all, gates))
    else:
        split = lambda v: v.reshape((chunks, v.shape[0] // chunks) + v.shape[1:])
        combined = lax.map(mix, (split(latent), split(base_all), split(gates)))
    combined = combined.reshape(owners, sub, hidden_all)

    if owners > LINE_MAX:
        mixed = lax.all_to_all(combined.astype(BF), "expert", 0, 0, tiled=True)
        own = jnp.sum(mixed.astype(F32), axis=0)
    else:
        own = scatter_sum(lambda index: lax.dynamic_index_in_dim(combined, index, 0, keepdims=False), "expert")
    full = direct_gather(direct_gather(own.astype(BF)[None], "tensor"), "inner")
    full = full.reshape(inners, tensors, sub, hidden_all).swapaxes(0, 1).reshape(rows, hidden_all)
    return dot(full, down_all, ((1,), (0,))).astype(BF)


def solution(mesh):
    return jax.shard_map(
        on_device,
        mesh=mesh,
        in_specs=(
            P(("groups", "expert"), ("tensor", "inner")),
            P(("groups", "expert"), None),
            P(("groups", "expert"), None),
            P(None, "expert", ("tensor", "inner")),
            P("expert", ("tensor", "inner")),
            P(None, "expert", ("tensor", "inner")),
            P("expert"),
        ),
        out_specs=P(("groups", "expert"), ("tensor", "inner")),
        check_vma=False,
    )
```

time: 664 us -> 190 us (0.29); the launches traced: 655 us -> 189 us
  waiting for transfers between devices: 486 us -> 44.6 us
  starting transfers between devices: 11.4 us -> 73.8 us
  local copies, waits for them, and re-layouts: 82.3 us -> 34.7 us
  between operations: 30.5 us -> 0.62 us
  matrix products: 31.7 us -> 14.1 us
  other arithmetic: 7.15 us -> 20.8 us
    all_to_all x2 -> x0, waiting for transfers between devices: 219 us -> none  [the longest x1 219 us: on_device(): lax.all_to_all(outgoing, 'expert', split_axis=1, concat_axis=1, tiled=True)]
    all_gather x1 -> x0, waiting for transfers between devices: 180 us -> none  [on_device(): gathered = lax.all_gather(base_weights, 'expert', axis=1, tiled=True)]
    ppermute x0 -> x33, starting transfers between devices: none -> 73.8 us  [the longest x9 46.5 us: chain_gather(): from_left = lax.ppermute(from_left, axis, up)]
    psum x1 -> x0, waiting for transfers between devices: 67.3 us -> none  [on_device(): summed = lax.psum(stacked.astype(jnp.bfloat16), ('tensor', 'inner'))]
    ppermute x0 -> x33, waiting for transfers between devices: none -> 44.6 us  [the longest x9 23 us: chain_gather(): from_left = lax.ppermute(from_left, axis, up)]
    scatter x1 -> x0, local copies, waits for them, and re-layouts: 31.4 us -> none  [on_device(): outgoing = outgoing.at[target].set(tokens[source_row])]
    reshape x3 -> x0, local copies, waits for them, and re-layouts: 30.3 us -> none  [the longest x1 20.6 us: on_device(): returned.reshape(local_count * owners * capacity, 2, hidden_slice)]
    reduce_scatter x1 -> x0, waiting for transfers between devices: 19.8 us -> none  [on_device(): lax.psum_scatter(partial_value.astype(jnp.bfloat16), ('tensor', 'inner'),...]
  transfers between devices with their start and end apart: 5 -> 33, of which waited for: 4 -> 12; matrix products, arithmetic and copies ran while one was open for 3% -> 33% of each run, Pallas kernels for 0% -> 0%
where the time goes in v1:
time: 190 us; the launch traced here: 189 us
  starting transfers between devices  73.8 us (39%)
  waiting for transfers between devices  44.6 us (23%)
  local copies, waits for them, and re-layouts  34.7 us (18%)
  other arithmetic  20.8 us (11%)
  matrix products  14.1 us (7%)
    ppermute x9, starting transfers between devices, chain_gather(): from_left = lax.ppermute(from_left, axis, up)  46.5 us
    ppermute x9, waiting for transfers between devices, chain_gather(): from_left = lax.ppermute(from_left, axis, up)  23 us
    unnamed x38, local copies, waits for them, and re-layouts  18.4 us
    dot_general x13, matrix products, dot(): lax.dot_general(lhs, rhs, (dims, ((), ())), preferred_element_type=F32)  14.1 us
    ppermute x9, starting transfers between devices, chain_gather(): from_right = lax.ppermute(from_right, axis, down)  11.9 us
    ppermute x8, waiting for transfers between devices, direct_gather(): lax.ppermute(value, axis, [(j, (j + shift) % size) for j in range(size)])  10.7 us
    concatenate x5, other arithmetic, direct_gather(): line = jnp.concatenate(got[:0:-1] + [value] + got[:0:-1], 0)  9.51 us
    ppermute x8, starting transfers between devices, direct_gather(): lax.ppermute(value, axis, [(j, (j + shift) % size) for j in range(size)])  8.83 us
  transfers between devices with their start and end apart: 33, of which 12 were waited for; matrix products, arithmetic and copies ran while one was open for 33% of the time, Pallas kernels for 0%

profile of v1, /device:TPU:0, one launch (start us, length us, event | category | flops | bytes accessed | tf_op | source)
XLA Modules:
  0.0 188.7 jit_solution(7749177165824376497)
XLA Ops:
  0.0 6.0 %collective-permute-start.3 = (bf16[128,1792]{1,0:T(8,128)(2,1)}, bf16[128,1792]{1,0:T(8,128)(2,1)}, u32[]{:S(2)}, u32[]{:S(2)}) collective-permute-start(bf16[128,1792]{1,0:T(8,128)(2,1)} %param.7), channel_id=1, source_target_pairs={{0,4},{4,8},{8,12},{1,5},{5,9},{9,13},{2,6},{6,10},{10,14},{3,7},{... | collective-permute-start | bytes 1376264 | tf_op jit(solution)/shard_map/ppermute | solution.py:24
  7.3 8.0 %collective-permute-done.3 = bf16[128,1792]{1,0:T(8,128)(2,1)} collective-permute-done((bf16[128,1792]{1,0:T(8,128)(2,1)}, bf16[128,1792]{1,0:T(8,128)(2,1)}, u32[]{:S(2)}, u32[]{:S(2)}) %collective-permute-start.3) | collective-permute-done | bytes 458784 | tf_op jit(solution)/shard_map/ppermute | solution.py:24
  15.3 5.2 %collective-permute-start.4 = (bf16[128,1792]{1,0:T(8,128)(2,1)}, bf16[128,1792]{1,0:T(8,128)(2,1)}, u32[]{:S(2)}, u32[]{:S(2)}) collective-permute-start(bf16[128,1792]{1,0:T(8,128)(2,1)} %collective-permute-done.3), channel_id=1, source_target_pairs={{0,4},{4,8},{8,12},{1,5},{5,9},{9,13},{2,6},{6,10},{10,14},{3,7},{... | collective-permute-start | bytes 1376264 | tf_op jit(solution)/shard_map/ppermute | solution.py:24
  23.5 5.5 %collective-permute-done.4 = bf16[128,1792]{1,0:T(8,128)(2,1)} collective-permute-done((bf16[128,1792]{1,0:T(8,128)(2,1)}, bf16[128,1792]{1,0:T(8,128)(2,1)}, u32[]{:S(2)}, u32[]{:S(2)}) %collective-permute-start.4) | collective-permute-done | bytes 458784 | tf_op jit(solution)/shard_map/ppermute | solution.py:24
  28.9 5.2 %collective-permute-start.5 = (bf16[128,1792]{1,0:T(8,128)(2,1)}, bf16[128,1792]{1,0:T(8,128)(2,1)}, u32[]{:S(2)}, u32[]{:S(2)}) collective-permute-start(bf16[128,1792]{1,0:T(8,128)(2,1)} %collective-permute-done.4), channel_id=1, source_target_pairs={{0,4},{4,8},{8,12},{1,5},{5,9},{9,13},{2,6},{6,10},{10,14},{3,7},{... | collective-permute-start | bytes 1376264 | tf_op jit(solution)/shard_map/ppermute | solution.py:24
  36.2 2.8 %collective-permute-start = (f32[32,32]{1,0:T(8,128)S(1)}, f32[32,32]{1,0:T(8,128)S(1)}, u32[]{:S(2)}, u32[]{:S(2)}) collective-permute-start(f32[32,32]{1,0:T(8,128)S(1)} %select_reduce_fusion.1), channel_id=1, source_target_pairs={{0,12},{4,0},{8,4},{12,8},{1,13},{5,1},{9,5},{13,9},{2,14},{6,2},{... | collective-permute-start | bytes 12296 | tf_op jit(solution)/shard_map/ppermute | solution.py:41
  39.0 2.2 %slice.47 = bf16[1,256,1792]{2,1,0:T(8,128)(2,1)} slice(bf16[3,256,1792]{2,1,0:T(8,128)(2,1)} %param.10), slice={[2:3], [0:256], [0:1792]} | slice | bytes 1835008 | tf_op jit(solution)/shard_map/slice | solution.py:111
  41.2 2.9 %slice.36 = bf16[2,256,1792]{2,1,0:T(8,128)(2,1)} slice(bf16[3,256,1792]{2,1,0:T(8,128)(2,1)} %param.10), slice={[0:2], [0:256], [0:1792]} | slice | bytes 3670016 | tf_op jit(solution)/shard_map/slice | solution.py:91
  44.3 1.9 dynamic-slice_bitcast_fusion.2
  54.3 4.6 %collective-permute-done.8 = bf16[128,1792]{1,0:T(8,128)(2,1)S(1)} collective-permute-done((bf16[128,1792]{1,0:T(8,128)(2,1)}, bf16[128,1792]{1,0:T(8,128)(2,1)S(1)}, u32[]{:S(2)}, u32[]{:S(2)}) %collective-permute-start.8) | collective-permute-done | bytes 458784 | tf_op jit(solution)/shard_map/ppermute | solution.py:25
  61.6 1.9 %convolution_convert_fusion.9 = bf16[256,960]{0,1:T(8,128)(2,1)} fusion(bf16[256,1792]{1,0:T(8,128)(2,1)S(1)} %bitcast.168, bf16[960,1792]{1,0:T(8,128)(2,1)S(1)} %copy-done), kind=kOutput, calls=%fused_computation.33 | convolution fusion | flops 881049600 | bytes 4849664 | tf_op jit(solution)/shard_map/dot_general | solution.py:12
  68.4 5.3 %collective-permute-start.26 = (bf16[1,128,1792]{2,1,0:T(8,128)(2,1)}, bf16[1,128,1792]{2,1,0:T(8,128)(2,1)}, u32[]{:S(2)}, u32[]{:S(2)}) collective-permute-start(bf16[1,128,1792]{2,1,0:T(8,128)(2,1)} %bitcast.157), channel_id=1, source_target_pairs={{0,4},{4,8},{8,12},{1,5},{5,9},{9,13},{2,6},{6,10},{10,14},{3,7},{... | collective-permute-start | bytes 1376264 | tf_op jit(solution)/shard_map/ppermute | solution.py:24
  73.7 1.7 fusion.14
  75.4 1.6 convert_element_type.167
  78.3 5.2 %collective-permute-start.11 = (bf16[1,128,2,256]{3,2,1,0:T(2,128)(2,1)}, bf16[1,128,2,256]{3,2,1,0:T(2,128)(2,1)}, u32[]{:S(2)}, u32[]{:S(2)}) collective-permute-start(bf16[1,128,2,256]{3,2,1,0:T(2,128)(2,1)} %convert_element_type.167), channel_id=1, source_target_pairs={{0,4},{4,8},{8,12},{1,5},{5,9},{9,13},{2,6},{6,10},{10,14},{3,7},{... | collective-permute-start | bytes 393224 | tf_op jit(solution)/shard_map/ppermute | solution.py:24
  83.5 3.3 %convert_add_fusion = f32[256,960]{0,1:T(8,128)} fusion(bf16[256,960]{0,1:T(8,128)(2,1)} %collective-permute-done.17, bf16[256,1792]{1,0:T(8,128)(2,1)} %bitcast.144, bf16[960,1792]{1,0:T(8,128)(2,1)S(1)} %copy-done), kind=kOutput, calls=%fused_computation.35 | convolution fusion | flops 881295360 | bytes 5832704 | tf_op jit(solution)/shard_map/dot_general | solution.py:12
  88.5 1.5 collective-permute-start.18
  91.5 4.6 %collective-permute-start.12 = (bf16[1,128,2,256]{3,2,1,0:T(2,128)(2,1)}, bf16[1,128,2,256]{3,2,1,0:T(2,128)(2,1)S(1)}, u32[]{:S(2)}, u32[]{:S(2)}) collective-permute-start(bf16[1,128,2,256]{3,2,1,0:T(2,128)(2,1)} %collective-permute-done.11), channel_id=1, source_target_pairs={{0,4},{4,8},{8,12},{1,5},{5,9},{9,13},{2,6},{6,10},{10,14},{3,7},{... | collective-permute-start | bytes 393224 | tf_op jit(solution)/shard_map/ppermute | solution.py:24
  96.1 2.6 %fusion.7 = bf16[2,2,960,256]{3,2,1,0:T(8,128)(2,1)S(1)} fusion(s32[]{:T(128)S(6)} %select_n.160, bf16[1,2,960,256]{3,2,1,0:T(8,128)(2,1)} %collective-permute-done.19, bf16[1,2,960,256]{3,2,1,0:T(8,128)(2,1)} %bitcast.166), kind=kLoop, calls=%fused_computation.23 | loop fusion | flops 1966080 | bytes 3932164 | tf_op jit(solution)/shard_map/concatenate | solution.py:43
  100.1 5.3 %collective-permute-start.27 = (bf16[1,128,1792]{2,1,0:T(8,128)(2,1)}, bf16[1,128,1792]{2,1,0:T(8,128)(2,1)}, u32[]{:S(2)}, u32[]{:S(2)}) collective-permute-start(bf16[1,128,1792]{2,1,0:T(8,128)(2,1)} %collective-permute-done.26), channel_id=1, source_target_pairs={{0,4},{4,8},{8,12},{1,5},{5,9},{9,13},{2,6},{6,10},{10,14},{3,7},{... | collective-permute-start | bytes 1376264 | tf_op jit(solution)/shard_map/ppermute | solution.py:24
  106.8 4.6 %collective-permute-start.13 = (bf16[1,128,2,256]{3,2,1,0:T(2,128)(2,1)S(1)}, bf16[1,128,2,256]{3,2,1,0:T(2,128)(2,1)S(1)}, u32[]{:S(2)}, u32[]{:S(2)}) collective-permute-start(bf16[1,128,2,256]{3,2,1,0:T(2,128)(2,1)S(1)} %collective-permute-done.12), channel_id=1, source_target_pairs={{0,4},{4,8},{8,12},{1,5},{5,9},{9,13},{2,6},{6,10},{10,14},{3,7},{... | collective-permute-start | bytes 393224 | tf_op jit(solution)/shard_map/ppermute | solution.py:24
  112.9 4.9 %collective-permute-done.13 = bf16[1,128,2,256]{3,2,1,0:T(2,128)(2,1)S(1)} collective-permute-done((bf16[1,128,2,256]{3,2,1,0:T(2,128)(2,1)S(1)}, bf16[1,128,2,256]{3,2,1,0:T(2,128)(2,1)S(1)}, u32[]{:S(2)}, u32[]{:S(2)}) %collective-permute-start.13) | collective-permute-done | bytes 131104 | tf_op jit(solution)/shard_map/ppermute | solution.py:24
  120.3 5.2 %collective-permute-start.28 = (bf16[1,128,1792]{2,1,0:T(8,128)(2,1)}, bf16[1,128,1792]{2,1,0:T(8,128)(2,1)}, u32[]{:S(2)}, u32[]{:S(2)}) collective-permute-start(bf16[1,128,1792]{2,1,0:T(8,128)(2,1)} %collective-permute-done.27), channel_id=1, source_target_pairs={{0,4},{4,8},{8,12},{1,5},{5,9},{9,13},{2,6},{6,10},{10,14},{3,7},{... | collective-permute-start | bytes 1376264 | tf_op jit(solution)/shard_map/ppermute | solution.py:24
  129.6 4.6 %collective-permute-done.28 = bf16[1,128,1792]{2,1,0:T(8,128)(2,1)} collective-permute-done((bf16[1,128,1792]{2,1,0:T(8,128)(2,1)}, bf16[1,128,1792]{2,1,0:T(8,128)(2,1)}, u32[]{:S(2)}, u32[]{:S(2)}) %collective-permute-start.28) | collective-permute-done | bytes 458784 | tf_op jit(solution)/shard_map/ppermute | solution.py:24
  144.7 3.1 %fusion.3 = bf16[4,2,960,256]{3,2,1,0:T(8,128)(2,1)S(1)} fusion(s32[]{:T(128)S(6)} %select_n.161, bf16[2,2,960,256]{3,2,1,0:T(8,128)(2,1)} %collective-permute-done.20, bf16[2,2,960,256]{3,2,1,0:T(8,128)(2,1)S(1)} %fusion.7), kind=kLoop, calls=%fused_computation.14 | loop fusion | flops 3932160 | bytes 7864324 | tf_op jit(solution)/shard_map/concatenate | solution.py:43
  157.0 5.4 %select_reduce_fusion = f32[128,1024]{0,1:T(8,128)S(1)} fusion(f32[8,128]{1,0:T(8,128)S(1)} %get-tuple-element.8, pred[8,128]{1,0:T(8,128)(4,1)S(1)} %get-tuple-element.7, f32[128,8,8,128]{3,2,1,0:T(8,128)S(1)} %copy.63, f32[128,1024]{0,1:T(8,128)S(1)} %get-tuple-element.15, f32[128,8,8,128]{3,2,1,0:T(8,128)S(1)} %copy.62, f32[128,1024]{0,1:T(8,128)S(1)} %get-tuple-element.14), kind=kLoop, calls=%fused_computation.12 | loop fusion | flops 12451840 | bytes 9966592 | tf_op jit(solution)/shard_map/reduce_sum | solution.py:144
  164.1 2.5 %collective-permute-start.23 = (bf16[32,1024]{1,0:T(8,128)(2,1)S(1)}, bf16[32,1024]{1,0:T(8,128)(2,1)S(1)}, u32[]{:S(2)}, u32[]{:S(2)}) collective-permute-start(bf16[32,1024]{1,0:T(8,128)(2,1)S(1)} %get-tuple-element.12), channel_id=1, source_target_pairs={{0,12},{4,0},{8,4},{12,8},{1,13},{5,1},{9,5},{13,9},{2,14},{6,2},{... | collective-permute-start | bytes 196616 | tf_op jit(solution)/shard_map/ppermute | solution.py:53
  166.5 2.4 %collective-permute-done.21 = bf16[32,1024]{1,0:T(8,128)(2,1)S(1)} collective-permute-done((bf16[32,1024]{1,0:T(8,128)(2,1)S(1)}, bf16[32,1024]{1,0:T(8,128)(2,1)S(1)}, u32[]{:S(2)}, u32[]{:S(2)}) %collective-permute-start.21) | collective-permute-done | bytes 65568 | tf_op jit(solution)/shard_map/ppermute | solution.py:53
  169.5 2.2 %collective-permute-done.22 = bf16[32,1024]{1,0:T(8,128)(2,1)S(1)} collective-permute-done((bf16[32,1024]{1,0:T(8,128)(2,1)S(1)}, bf16[32,1024]{1,0:T(8,128)(2,1)S(1)}, u32[]{:S(2)}, u32[]{:S(2)}) %collective-permute-start.22) | collective-permute-done | bytes 65568 | tf_op jit(solution)/shard_map/ppermute | solution.py:53
  172.6 3.4 %collective-permute-done.24 = bf16[1,32,1024]{2,1,0:T(8,128)(2,1)S(1)} collective-permute-done((bf16[1,32,1024]{2,1,0:T(8,128)(2,1)S(1)}, bf16[1,32,1024]{2,1,0:T(8,128)(2,1)S(1)}, u32[]{:S(2)}, u32[]{:S(2)}) %collective-permute-start.24) | collective-permute-done | bytes 65568 | tf_op jit(solution)/shard_map/ppermute | solution.py:41
  177.7 5.9 %collective-permute-done.32 = bf16[1,4,128,1792]{3,2,0,1:T(8,128)(2,1)} collective-permute-done((bf16[1,4,128,1792]{3,2,0,1:T(8,128)(2,1)}, bf16[1,4,128,1792]{3,2,0,1:T(8,128)(2,1)}, u32[]{:S(2)}, u32[]{:S(2)}) %collective-permute-start.32) | collective-permute-done | bytes 1835040 | tf_op jit(solution)/shard_map/ppermute | solution.py:41
  183.6 3.6 %fusion.5 = bf16[2,4,128,1792]{3,2,0,1:T(8,128)(2,1)S(1)} fusion(s32[]{:T(128)S(6)} %select_n.171, bf16[1,4,128,1792]{3,2,0,1:T(8,128)(2,1)} %collective-permute-done.32, bf16[1,4,128,1792]{3,2,0,1:T(8,128)(2,1)} %dynamic-slice_bitcast_fusion), kind=kLoop, calls=%fused_computation.16 | loop fusion | flops 3670016 | bytes 7340036 | tf_op jit(solution)/shard_map/concatenate | solution.py:43
  (130 shorter events, 62.9 us)
Async XLA Ops:
  0.0 15.3 %collective-permute-start.3 = (bf16[128,1792]{1,0:T(8,128)(2,1)}, bf16[128,1792]{1,0:T(8,128)(2,1)}, u32[]{:S(2)}, u32[]{:S(2)}) collective-permute-start(bf16[128,1792]{1,0:T(8,128)(2,1)} %param.7), channel_id=1, source_target_pairs={{0,4},{4,8},{8,12},{1,5},{5,9},{9,13},{2,6},{6,10},{10,14},{3,7},{... | collective-permute-start | bytes 1376264 | tf_op jit(solution)/shard_map/ppermute | solution.py:24
  6.0 16.1 %collective-permute-start.6 = (bf16[128,1792]{1,0:T(8,128)(2,1)}, bf16[128,1792]{1,0:T(8,128)(2,1)}, u32[]{:S(2)}, u32[]{:S(2)}) collective-permute-start(bf16[128,1792]{1,0:T(8,128)(2,1)} %param.7), channel_id=1, source_target_pairs={{4,0},{8,4},{12,8},{5,1},{9,5},{13,9},{6,2},{10,6},{14,10},{7,3},{... | collective-permute-start | bytes 1376264 | tf_op jit(solution)/shard_map/ppermute | solution.py:25
  15.3 13.6 %collective-permute-start.4 = (bf16[128,1792]{1,0:T(8,128)(2,1)}, bf16[128,1792]{1,0:T(8,128)(2,1)}, u32[]{:S(2)}, u32[]{:S(2)}) collective-permute-start(bf16[128,1792]{1,0:T(8,128)(2,1)} %collective-permute-done.3), channel_id=1, source_target_pairs={{0,4},{4,8},{8,12},{1,5},{5,9},{9,13},{2,6},{6,10},{10,14},{3,7},{... | collective-permute-start | bytes 1376264 | tf_op jit(solution)/shard_map/ppermute | solution.py:24
  22.2 24.0 %collective-permute-start.7 = (bf16[128,1792]{1,0:T(8,128)(2,1)}, bf16[128,1792]{1,0:T(8,128)(2,1)}, u32[]{:S(2)}, u32[]{:S(2)}) collective-permute-start(bf16[128,1792]{1,0:T(8,128)(2,1)} %collective-permute-done.6), channel_id=1, source_target_pairs={{4,0},{8,4},{12,8},{5,1},{9,5},{13,9},{6,2},{10,6},{14,10},{7,3},{... | collective-permute-start | bytes 1376264 | tf_op jit(solution)/shard_map/ppermute | solution.py:25
  28.9 18.8 %collective-permute-start.5 = (bf16[128,1792]{1,0:T(8,128)(2,1)}, bf16[128,1792]{1,0:T(8,128)(2,1)}, u32[]{:S(2)}, u32[]{:S(2)}) collective-permute-start(bf16[128,1792]{1,0:T(8,128)(2,1)} %collective-permute-done.4), channel_id=1, source_target_pairs={{0,4},{4,8},{8,12},{1,5},{5,9},{9,13},{2,6},{6,10},{10,14},{3,7},{... | collective-permute-start | bytes 1376264 | tf_op jit(solution)/shard_map/ppermute | solution.py:24
  34.2 31.9 %collective-permute-start.2 = (f32[32,32]{1,0:T(8,128)S(1)}, f32[32,32]{1,0:T(8,128)S(1)}, u32[]{:S(2)}, u32[]{:S(2)}) collective-permute-start(f32[32,32]{1,0:T(8,128)S(1)} %select_reduce_fusion.1), channel_id=1, source_target_pairs={{0,4},{4,8},{8,12},{12,0},{1,5},{5,9},{9,13},{13,1},{2,6},{6,10},{... | collective-permute-start | bytes 12296 | tf_op jit(solution)/shard_map/ppermute | solution.py:41
  35.1 31.8 %collective-permute-start.1 = (f32[32,32]{1,0:T(8,128)S(1)}, f32[32,32]{1,0:T(8,128)S(1)}, u32[]{:S(2)}, u32[]{:S(2)}) collective-permute-start(f32[32,32]{1,0:T(8,128)S(1)} %select_reduce_fusion.1), channel_id=1, source_target_pairs={{0,8},{4,12},{8,0},{12,4},{1,9},{5,13},{9,1},{13,5},{2,10},{6,14},... | collective-permute-start | bytes 12296 | tf_op jit(solution)/shard_map/ppermute | solution.py:41
  36.2 30.8 %collective-permute-start = (f32[32,32]{1,0:T(8,128)S(1)}, f32[32,32]{1,0:T(8,128)S(1)}, u32[]{:S(2)}, u32[]{:S(2)}) collective-permute-start(f32[32,32]{1,0:T(8,128)S(1)} %select_reduce_fusion.1), channel_id=1, source_target_pairs={{0,12},{4,0},{8,4},{12,8},{1,13},{5,1},{9,5},{13,9},{2,14},{6,2},{... | collective-permute-start | bytes 12296 | tf_op jit(solution)/shard_map/ppermute | solution.py:41
  46.2 42.3 %collective-permute-start.19 = (bf16[1,2,960,256]{3,2,1,0:T(8,128)(2,1)}, bf16[1,2,960,256]{3,2,1,0:T(8,128)(2,1)}, u32[]{:S(2)}, u32[]{:S(2)}) collective-permute-start(bf16[1,2,960,256]{3,2,1,0:T(8,128)(2,1)} %bitcast.165), channel_id=1, source_target_pairs={{0,2},{2,0},{1,3},{3,1},{4,6},{6,4},{5,7},{7,5},{8,10},{10,8},{9,1... | collective-permute-start | bytes 2949128 | tf_op jit(solution)/shard_map/ppermute | solution.py:41
  47.7 11.2 %collective-permute-start.8 = (bf16[128,1792]{1,0:T(8,128)(2,1)}, bf16[128,1792]{1,0:T(8,128)(2,1)S(1)}, u32[]{:S(2)}, u32[]{:S(2)}) collective-permute-start(bf16[128,1792]{1,0:T(8,128)(2,1)} %collective-permute-done.7), channel_id=1, source_target_pairs={{4,0},{8,4},{12,8},{5,1},{9,5},{13,9},{6,2},{10,6},{14,10},{7,3},{... | collective-permute-start | bytes 1376264 | tf_op jit(solution)/shard_map/ppermute | solution.py:25
  61.5 2.0 %collective-permute-start.9 = (bf16[256,512]{1,0:T(8,128)(2,1)S(1)}, bf16[256,512]{1,0:T(8,128)(2,1)S(1)}, u32[]{:S(2)}, u32[]{:S(2)}) collective-permute-start(bf16[256,512]{1,0:T(8,128)(2,1)S(1)} %convolution_convert_fusion.10), channel_id=1, source_target_pairs={{0,1},{1,0},{2,3},{3,2},{4,5},{5,4},{6,7},{7,6},{8,9},{9,8},{10,11... | collective-permute-start | bytes 786440 | tf_op jit(solution)/shard_map/ppermute | solution.py:53
  63.5 14.9 %collective-permute-start.17 = (bf16[256,960]{0,1:T(8,128)(2,1)}, bf16[256,960]{0,1:T(8,128)(2,1)}, u32[]{:S(2)}, u32[]{:S(2)}) collective-permute-start(bf16[256,960]{0,1:T(8,128)(2,1)} %convolution_convert_fusion.9), channel_id=1, source_target_pairs={{0,1},{1,0},{2,3},{3,2},{4,5},{5,4},{6,7},{7,6},{8,9},{9,8},{10,11... | collective-permute-start | bytes 1474568 | tf_op jit(solution)/shard_map/ppermute | solution.py:53
  66.1 7.6 %collective-permute-start.10 = (bf16[4,32,512]{2,1,0:T(8,128)(2,1)}, bf16[4,32,512]{2,1,0:T(8,128)(2,1)}, u32[]{:S(2)}, u32[]{:S(2)}) collective-permute-start(bf16[4,32,512]{2,1,0:T(8,128)(2,1)} %fusion.17), channel_id=1, source_target_pairs={{0,2},{2,0},{1,3},{3,1},{4,6},{6,4},{5,7},{7,5},{8,10},{10,8},{9,1... | collective-permute-start | bytes 393224 | tf_op jit(solution)/shard_map/ppermute | solution.py:53
  67.1 31.6 %collective-permute-start.29 = (bf16[1,128,1792]{2,1,0:T(8,128)(2,1)}, bf16[1,128,1792]{2,1,0:T(8,128)(2,1)}, u32[]{:S(2)}, u32[]{:S(2)}) collective-permute-start(bf16[1,128,1792]{2,1,0:T(8,128)(2,1)} %bitcast.156), channel_id=1, source_target_pairs={{4,0},{8,4},{12,8},{5,1},{9,5},{13,9},{6,2},{10,6},{14,10},{7,3},{... | collective-permute-start | bytes 1376264 | tf_op jit(solution)/shard_map/ppermute | solution.py:25
  68.4 30.4 %collective-permute-start.26 = (bf16[1,128,1792]{2,1,0:T(8,128)(2,1)}, bf16[1,128,1792]{2,1,0:T(8,128)(2,1)}, u32[]{:S(2)}, u32[]{:S(2)}) collective-permute-start(bf16[1,128,1792]{2,1,0:T(8,128)(2,1)} %bitcast.157), channel_id=1, source_target_pairs={{0,4},{4,8},{8,12},{1,5},{5,9},{9,13},{2,6},{6,10},{10,14},{3,7},{... | collective-permute-start | bytes 1376264 | tf_op jit(solution)/shard_map/ppermute | solution.py:24
  77.0 13.1 %collective-permute-start.14 = (bf16[1,128,2,256]{3,2,1,0:T(2,128)(2,1)}, bf16[1,128,2,256]{3,2,1,0:T(2,128)(2,1)}, u32[]{:S(2)}, u32[]{:S(2)}) collective-permute-start(bf16[1,128,2,256]{3,2,1,0:T(2,128)(2,1)} %convert_element_type.167), channel_id=1, source_target_pairs={{4,0},{8,4},{12,8},{5,1},{9,5},{13,9},{6,2},{10,6},{14,10},{7,3},{... | collective-permute-start | bytes 393224 | tf_op jit(solution)/shard_map/ppermute | solution.py:25
  78.3 13.2 %collective-permute-start.11 = (bf16[1,128,2,256]{3,2,1,0:T(2,128)(2,1)}, bf16[1,128,2,256]{3,2,1,0:T(2,128)(2,1)}, u32[]{:S(2)}, u32[]{:S(2)}) collective-permute-start(bf16[1,128,2,256]{3,2,1,0:T(2,128)(2,1)} %convert_element_type.167), channel_id=1, source_target_pairs={{0,4},{4,8},{8,12},{1,5},{5,9},{9,13},{2,6},{6,10},{10,14},{3,7},{... | collective-permute-start | bytes 393224 | tf_op jit(solution)/shard_map/ppermute | solution.py:24
  88.5 18.3 %collective-permute-start.18 = (bf16[4,32,960]{2,1,0:T(8,128)(2,1)S(1)}, bf16[4,32,960]{2,1,0:T(8,128)(2,1)S(1)}, u32[]{:S(2)}, u32[]{:S(2)}) collective-permute-start(bf16[4,32,960]{2,1,0:T(8,128)(2,1)S(1)} %fusion.11), channel_id=1, source_target_pairs={{0,2},{2,0},{1,3},{3,1},{4,6},{6,4},{5,7},{7,5},{8,10},{10,8},{9,1... | collective-permute-start | bytes 737288 | tf_op jit(solution)/shard_map/ppermute | solution.py:53
  90.1 10.0 %collective-permute-start.15 = (bf16[1,128,2,256]{3,2,1,0:T(2,128)(2,1)}, bf16[1,128,2,256]{3,2,1,0:T(2,128)(2,1)S(1)}, u32[]{:S(2)}, u32[]{:S(2)}) collective-permute-start(bf16[1,128,2,256]{3,2,1,0:T(2,128)(2,1)} %collective-permute-done.14), channel_id=1, source_target_pairs={{4,0},{8,4},{12,8},{5,1},{9,5},{13,9},{6,2},{10,6},{14,10},{7,3},{... | collective-permute-start | bytes 393224 | tf_op jit(solution)/shard_map/ppermute | solution.py:25
  91.5 13.9 %collective-permute-start.12 = (bf16[1,128,2,256]{3,2,1,0:T(2,128)(2,1)}, bf16[1,128,2,256]{3,2,1,0:T(2,128)(2,1)S(1)}, u32[]{:S(2)}, u32[]{:S(2)}) collective-permute-start(bf16[1,128,2,256]{3,2,1,0:T(2,128)(2,1)} %collective-permute-done.11), channel_id=1, source_target_pairs={{0,4},{4,8},{8,12},{1,5},{5,9},{9,13},{2,6},{6,10},{10,14},{3,7},{... | collective-permute-start | bytes 393224 | tf_op jit(solution)/shard_map/ppermute | solution.py:24
  98.7 46.0 %collective-permute-start.20 = (bf16[2,2,960,256]{3,2,1,0:T(8,128)(2,1)S(1)}, bf16[2,2,960,256]{3,2,1,0:T(8,128)(2,1)}, u32[]{:S(2)}, u32[]{:S(2)}) collective-permute-start(bf16[2,2,960,256]{3,2,1,0:T(8,128)(2,1)S(1)} %fusion.7), channel_id=1, source_target_pairs={{0,1},{1,0},{2,3},{3,2},{4,5},{5,4},{6,7},{7,6},{8,9},{9,8},{10,11... | collective-permute-start | bytes 5898248 | tf_op jit(solution)/shard_map/ppermute | solution.py:41
  98.8 29.3 %collective-permute-start.30 = (bf16[1,128,1792]{2,1,0:T(8,128)(2,1)}, bf16[1,128,1792]{2,1,0:T(8,128)(2,1)}, u32[]{:S(2)}, u32[]{:S(2)}) collective-permute-start(bf16[1,128,1792]{2,1,0:T(8,128)(2,1)} %collective-permute-done.29), channel_id=1, source_target_pairs={{4,0},{8,4},{12,8},{5,1},{9,5},{13,9},{6,2},{10,6},{14,10},{7,3},{... | collective-permute-start | bytes 1376264 | tf_op jit(solution)/shard_map/ppermute | solution.py:25
  100.1 20.2 %collective-permute-start.27 = (bf16[1,128,1792]{2,1,0:T(8,128)(2,1)}, bf16[1,128,1792]{2,1,0:T(8,128)(2,1)}, u32[]{:S(2)}, u32[]{:S(2)}) collective-permute-start(bf16[1,128,1792]{2,1,0:T(8,128)(2,1)} %collective-permute-done.26), channel_id=1, source_target_pairs={{0,4},{4,8},{8,12},{1,5},{5,9},{9,13},{2,6},{6,10},{10,14},{3,7},{... | collective-permute-start | bytes 1376264 | tf_op jit(solution)/shard_map/ppermute | solution.py:24
  105.5 20.0 %collective-permute-start.16 = (bf16[1,128,2,256]{3,2,1,0:T(2,128)(2,1)S(1)}, bf16[1,128,2,256]{3,2,1,0:T(2,128)(2,1)S(1)}, u32[]{:S(2)}, u32[]{:S(2)}) collective-permute-start(bf16[1,128,2,256]{3,2,1,0:T(2,128)(2,1)S(1)} %collective-permute-done.15), channel_id=1, source_target_pairs={{4,0},{8,4},{12,8},{5,1},{9,5},{13,9},{6,2},{10,6},{14,10},{7,3},{... | collective-permute-start | bytes 393224 | tf_op jit(solution)/shard_map/ppermute | solution.py:25
  106.8 11.1 %collective-permute-start.13 = (bf16[1,128,2,256]{3,2,1,0:T(2,128)(2,1)S(1)}, bf16[1,128,2,256]{3,2,1,0:T(2,128)(2,1)S(1)}, u32[]{:S(2)}, u32[]{:S(2)}) collective-permute-start(bf16[1,128,2,256]{3,2,1,0:T(2,128)(2,1)S(1)} %collective-permute-done.12), channel_id=1, source_target_pairs={{0,4},{4,8},{8,12},{1,5},{5,9},{9,13},{2,6},{6,10},{10,14},{3,7},{... | collective-permute-start | bytes 393224 | tf_op jit(solution)/shard_map/ppermute | solution.py:24
  120.3 14.0 %collective-permute-start.28 = (bf16[1,128,1792]{2,1,0:T(8,128)(2,1)}, bf16[1,128,1792]{2,1,0:T(8,128)(2,1)}, u32[]{:S(2)}, u32[]{:S(2)}) collective-permute-start(bf16[1,128,1792]{2,1,0:T(8,128)(2,1)} %collective-permute-done.27), channel_id=1, source_target_pairs={{0,4},{4,8},{8,12},{1,5},{5,9},{9,13},{2,6},{6,10},{10,14},{3,7},{... | collective-permute-start | bytes 1376264 | tf_op jit(solution)/shard_map/ppermute | solution.py:24
  128.1 13.6 %collective-permute-start.31 = (bf16[1,128,1792]{2,1,0:T(8,128)(2,1)}, bf16[1,128,1792]{2,1,0:T(8,128)(2,1)S(1)}, u32[]{:S(2)}, u32[]{:S(2)}) collective-permute-start(bf16[1,128,1792]{2,1,0:T(8,128)(2,1)} %collective-permute-done.30), channel_id=1, source_target_pairs={{4,0},{8,4},{12,8},{5,1},{9,5},{13,9},{6,2},{10,6},{14,10},{7,3},{... | collective-permute-start | bytes 1376264 | tf_op jit(solution)/shard_map/ppermute | solution.py:25
  143.1 40.4 %collective-permute-start.32 = (bf16[1,4,128,1792]{3,2,0,1:T(8,128)(2,1)}, bf16[1,4,128,1792]{3,2,0,1:T(8,128)(2,1)}, u32[]{:S(2)}, u32[]{:S(2)}) collective-permute-start(bf16[1,4,128,1792]{3,2,0,1:T(8,128)(2,1)} %dynamic-slice_bitcast_fusion), channel_id=1, source_target_pairs={{0,16},{16,0},{1,17},{17,1},{2,18},{18,2},{3,19},{19,3},{4,20},{20... | collective-permute-start | bytes 5505032 | tf_op jit(solution)/shard_map/ppermute | solution.py:41
  162.7 6.3 %collective-permute-start.21 = (bf16[32,1024]{1,0:T(8,128)(2,1)S(1)}, bf16[32,1024]{1,0:T(8,128)(2,1)S(1)}, u32[]{:S(2)}, u32[]{:S(2)}) collective-permute-start(bf16[32,1024]{1,0:T(8,128)(2,1)S(1)} %get-tuple-element.11), channel_id=1, source_target_pairs={{0,4},{4,8},{8,12},{12,0},{1,5},{5,9},{9,13},{13,1},{2,6},{6,10},{... | collective-permute-start | bytes 196616 | tf_op jit(solution)/shard_map/ppermute | solution.py:53
  164.1 5.4 %collective-permute-start.23 = (bf16[32,1024]{1,0:T(8,128)(2,1)S(1)}, bf16[32,1024]{1,0:T(8,128)(2,1)S(1)}, u32[]{:S(2)}, u32[]{:S(2)}) collective-permute-start(bf16[32,1024]{1,0:T(8,128)(2,1)S(1)} %get-tuple-element.12), channel_id=1, source_target_pairs={{0,12},{4,0},{8,4},{12,8},{1,13},{5,1},{9,5},{13,9},{2,14},{6,2},{... | collective-permute-start | bytes 196616 | tf_op jit(solution)/shard_map/ppermute | solution.py:53
  166.5 5.2 %collective-permute-start.22 = (bf16[32,1024]{1,0:T(8,128)(2,1)S(1)}, bf16[32,1024]{1,0:T(8,128)(2,1)S(1)}, u32[]{:S(2)}, u32[]{:S(2)}) collective-permute-start(bf16[32,1024]{1,0:T(8,128)(2,1)S(1)} %get-tuple-element.13), channel_id=1, source_target_pairs={{0,8},{4,12},{8,0},{12,4},{1,9},{5,13},{9,1},{13,5},{2,10},{6,14},... | collective-permute-start | bytes 196616 | tf_op jit(solution)/shard_map/ppermute | solution.py:53
  171.7 4.3 %collective-permute-start.24 = (bf16[1,32,1024]{2,1,0:T(8,128)(2,1)S(1)}, bf16[1,32,1024]{2,1,0:T(8,128)(2,1)S(1)}, u32[]{:S(2)}, u32[]{:S(2)}) collective-permute-start(bf16[1,32,1024]{2,1,0:T(8,128)(2,1)S(1)} %fusion.24), channel_id=1, source_target_pairs={{0,2},{2,0},{1,3},{3,1},{4,6},{6,4},{5,7},{7,5},{8,10},{10,8},{9,1... | collective-permute-start | bytes 196616 | tf_op jit(solution)/shard_map/ppermute | solution.py:41
  (10 other events, 160.9 us)

commit v2 on v1

--- a/solution.py
+++ b/solution.py
@@ -1,6 +1,8 @@
 import jax
 import jax.numpy as jnp
 from jax import lax
+from jax.experimental import pallas as pl
+from jax.experimental.pallas import tpu as pltpu
 from jax.sharding import PartitionSpec as P
 
 BF = jnp.bfloat16
@@ -61,7 +63,7 @@
     return lax.optimization_barrier((value,) + others)[0]
 
 
-def on_device(tokens, expert_ids, gate_weights, base_weights, in_factor, out_factors, ranks):
+def general(tokens, expert_ids, gate_weights, base_weights, in_factor, out_factors, ranks):
     rows, feats = tokens.shape
     owners = lax.axis_size("expert")
     tensors, inners = lax.axis_size("tensor"), lax.axis_size("inner")
@@ -161,9 +163,218 @@
     return dot(full, down_all, ((1,), (0,))).astype(BF)
 
 
+def swaps(size, k):
+    return [(j, j ^ k) for j in range(size)]
+
+
+def pick(value, index, count, axis=0):
+    return lax.dynamic_slice_in_dim(value, index * count, count, axis)
+
+
+def pair_sum(parts, axis, rows):
+    index = lax.axis_index(axis)
+    half = rows // 2
+    sent = pick(parts, index ^ 1, half, 1).astype(BF)
+    got = lax.ppermute(sent, axis, swaps(2, 1))
+    return pick(parts, index, half, 1).astype(F32) + got.astype(F32)
+
+
+def gated_kernel(where_ref, *refs, slots, early, local, units, inner_units):
+    owners = slots
+    blocks = owners
+    tables_a = refs[:owners]
+    tables_b = refs[owners : 2 * owners]
+    deltas = refs[2 * owners : 2 * owners + 2 * blocks]
+    gates = refs[2 * owners + 2 * blocks]
+    out = refs[-1]
+    z = where_ref[0]
+    part = where_ref[1]
+
+    def table(j, k, g):
+        source = k ^ j
+        lo = g * units
+        if source < early:
+            return tables_a[j][source, :, lo : lo + units].astype(F32)
+        return tables_b[j][source - early, :, lo : lo + units].astype(F32)
+
+    for m in range(blocks):
+        h = part ^ m
+        j_of = z ^ h
+        for k in range(slots):
+            base = []
+            for g in range(2):
+                chosen = table(0, k, g)
+                for j in range(1, owners):
+                    chosen = jnp.where(j_of == j, table(j, k, g), chosen)
+                base.append(chosen)
+            total = jnp.zeros_like(base[0])
+            for e in range(local):
+                gate = base[0] + deltas[2 * m][e, k].astype(F32)
+                up = base[1] + deltas[2 * m + 1][e, k].astype(F32)
+                hidden = gate / (1.0 + jnp.exp(-gate)) * up
+                weight = gates[k, :, e : e + 1]
+                total = total + jnp.where(weight > 0, weight * hidden, 0.0)
+            total = total.astype(BF)
+            for q in range(units // inner_units):
+                out[k, h * (units // inner_units) + q] = total[:, q * inner_units : (q + 1) * inner_units]
+
+
+def final_kernel(where_ref, *refs, rows_of, weights_of, tile):
+    count = len(rows_of)
+    lhs = refs[:count]
+    rhs = refs[count:-1]
+    out = refs[-1]
+    sub = lhs[0].shape[1]
+    feats = out.shape[1]
+    left = []
+    for w, _ in weights_of:
+        index = where_ref[count + len(left)]
+        left.append(jnp.concatenate([p[index] for p in lhs], 0))
+    for lo in range(0, feats, tile):
+        total = None
+        for q, (w, row) in enumerate(weights_of):
+            piece = rhs[w][row : row + left[q].shape[1], lo : lo + tile]
+            term = lax.dot_general(left[q], piece, (((1,), (0,)), ((), ())), preferred_element_type=F32)
+            total = term if total is None else total + term
+        total = total.astype(BF)
+        for r in range(count):
+            start = pl.multiple_of(where_ref[r], sub)
+            out[pl.ds(start, sub), lo : lo + tile] = total[r * sub : (r + 1) * sub]
+
+
+def fast(tokens, expert_ids, gate_weights, base_weights, in_factor, out_factors, ranks):
+    rows, feats = tokens.shape
+    owners = lax.axis_size("expert")
+    tensors, inners = lax.axis_size("tensor"), lax.axis_size("inner")
+    copies = lax.axis_size("groups")
+    local = ranks.shape[0]
+    experts = local * owners
+    units = base_weights.shape[1]
+    width = in_factor.shape[0]
+    sub = rows // (tensors * inners)
+    z = lax.axis_index("expert")
+    t = lax.axis_index("tensor")
+    c = lax.axis_index("inner")
+    g = lax.axis_index("groups")
+    part = t * inners + c
+    rows_at = c * tensors + t
+    early = owners - 1
+
+    second = lax.ppermute(tokens, "expert", swaps(owners, 2))
+    first = lax.ppermute(tokens, "expert", swaps(owners, 1))
+
+    own_ids = pick(expert_ids, rows_at, sub)
+    own_gates = pick(gate_weights, rows_at, sub)
+    columns = lax.broadcasted_iota(jnp.int32, (1, 1, experts), 2)
+    dense = jnp.sum(jnp.where(own_ids[:, :, None] == columns, own_gates[:, :, None], 0.0), axis=1)
+    gates = [pick(dense, z, local, 1)]
+    for k in range(1, owners):
+        gates.append(lax.ppermute(pick(dense, z ^ k, local, 1), "expert", swaps(owners, k)))
+    gates = jnp.stack(gates)
+
+    across = lax.ppermute(out_factors, "tensor", swaps(tensors, 1))
+    factors = [
+        out_factors,
+        lax.ppermute(out_factors, "inner", swaps(inners, 1)),
+        across,
+        lax.ppermute(across, "inner", swaps(inners, 1)),
+    ]
+
+    forward = lax.ppermute(after(second, first), "expert", [(1, 0), (2, 3)])
+    middle = lax.ppermute(after(tokens, first, second), "expert", [(1, 2), (2, 1)])
+    third = jnp.where((z == 1) | (z == 2), middle, forward)
+
+    base_flat = base_weights[:2].reshape(2 * units, feats)
+
+    def product(value, weights):
+        parts = dot(value, weights, ((1,), (1,)))
+        parts = parts.reshape(value.shape[0] // rows, rows, weights.shape[0])
+        parts = pair_sum(parts, "inner", rows)
+        return pair_sum(parts, "tensor", rows // inners).astype(BF)
+
+    ready = jnp.concatenate([tokens, first, second], 0)
+    base_a = product(ready, base_flat)
+    latent_a = product(ready, in_factor)
+    base_b = product(third, base_flat)
+    latent_b = product(third, in_factor)
+
+    tables_a, tables_b = [base_a], [base_b]
+    for k in range(1, owners):
+        tables_a.append(lax.ppermute(base_a, "expert", swaps(owners, k)))
+    for k in range(1, owners):
+        tables_b.append(lax.ppermute(base_b, "expert", swaps(owners, k)))
+
+    down = base_weights[2]
+    piece = units // copies
+    mine = after(pick(down, g, piece), third)
+    near, far = [], []
+    for k in range(1, owners):
+        half = lax.ppermute(mine, "expert", swaps(owners, k))
+        near.append(half)
+        far.append(lax.ppermute(half, "groups", swaps(copies, 1)))
+
+    ends = jnp.cumsum(ranks)
+    position = lax.broadcasted_iota(jnp.int32, (1, width), 1)
+    owner_of = jnp.sum((position[:, :, None] >= ends[None, None, :]).astype(jnp.int32), axis=2)
+    member = lax.broadcasted_iota(jnp.int32, (local, 1, 1), 0)
+    latent = jnp.concatenate([latent_a, latent_b], 0).reshape(owners * sub, width)
+    spread = jnp.where(owner_of[None] == member, latent[None], jnp.zeros((), BF))
+    spread = spread.reshape(local * owners * sub, width)
+    deltas = []
+    for m in range(owners):
+        for side in range(2):
+            delta = dot(spread, factors[m][side], ((1,), (0,))).astype(BF)
+            deltas.append(delta.reshape(local, owners, sub, units))
+
+    spot = jnp.stack([z, part]).astype(jnp.int32)
+    whole = pl.BlockSpec(memory_space=pltpu.VMEM)
+    numbers = pl.BlockSpec(memory_space=pltpu.SMEM)
+    combined = pl.pallas_call(
+        lambda *refs: gated_kernel(
+            *refs, slots=owners, early=early, local=local, units=units, inner_units=piece
+        ),
+        out_shape=jax.ShapeDtypeStruct((owners, owners * copies, sub, piece), BF),
+        in_specs=[numbers] + [whole] * (2 * owners + 2 * owners + 1),
+        out_specs=whole,
+        name="gated",
+    )(spot, *tables_a, *tables_b, *deltas, gates)
+
+    total = combined[0].astype(F32)
+    for k in range(1, owners):
+        total = total + lax.ppermute(combined[k], "expert", swaps(owners, k)).astype(F32)
+    own = total.astype(BF)
+    beside = lax.ppermute(own, "tensor", swaps(tensors, 1))
+    lhs = [own, beside, lax.ppermute(own, "inner", swaps(inners, 1)), lax.ppermute(beside, "inner", swaps(inners, 1))]
+    starts = [
+        (c * tensors + t) * sub,
+        (c * tensors + (t ^ 1)) * sub,
+        ((c ^ 1) * tensors + t) * sub,
+        ((c ^ 1) * tensors + (t ^ 1)) * sub,
+    ]
+    rhs = [down] + near + far
+    weights_of = [(0, q * piece) for q in range(copies)]
+    order = [z * copies + q for q in range(copies)]
+    for k in range(1, owners):
+        weights_of.append((k, 0))
+        order.append((z ^ k) * copies + g)
+    for k in range(1, owners):
+        weights_of.append((owners - 1 + k, 0))
+        order.append((z ^ k) * copies + (g ^ 1))
+    spot = jnp.stack(starts + order).astype(jnp.int32)
+    return pl.pallas_call(
+        lambda *refs: final_kernel(*refs, rows_of=starts, weights_of=weights_of, tile=2 * piece),
+        out_shape=jax.ShapeDtypeStruct((rows, feats), BF),
+        in_specs=[numbers] + [whole] * (len(lhs) + len(rhs)),
+        out_specs=whole,
+        name="final",
+    )(spot, *lhs, *rhs)
+
+
 def solution(mesh):
+    shape = mesh.shape
+    small = shape["expert"] == 4 and shape["tensor"] == 2 and shape["inner"] == 2 and shape["groups"] == 2
     return jax.shard_map(
-        on_device,
+        fast if small else general,
         mesh=mesh,
         in_specs=(
             P(("groups", "expert"), ("tensor", "inner")),

time: 190 us -> 216 us (1.14)
  waiting for transfers between devices: 44.6 us -> 109 us
  starting transfers between devices: 73.8 us -> 40.6 us
  other arithmetic: 20.8 us -> 5.99 us
  matrix products: 14.1 us -> 24 us
  Pallas kernels: 0 us -> 9.36 us
  local copies, waits for them, and re-layouts: 34.7 us -> 26.1 us
    ppermute x33 -> x36, waiting for transfers between devices: 44.6 us -> 109 us  [the longest x3 37.7 us: fast(): tables_b.append(lax.ppermute(base_b, 'expert', swaps(owners, k)))]
    ppermute x33 -> x36, starting transfers between devices: 73.8 us -> 40.6 us  [the longest x3 6.19 us: fast(): tables_a.append(lax.ppermute(base_a, 'expert', swaps(owners, k)))]
    unnamed x38 -> x33, local copies, waits for them, and re-layouts: 18.4 us -> 6.68 us
    dot_general x13 -> x12, matrix products: 14.1 us -> 24 us  [dot(): lax.dot_general(lhs, rhs, (dims, ((), ())), preferred_element_type=F32)]
    concatenate x5 -> x1, other arithmetic: 9.51 us -> 0.03 us  [fast(): jnp.concatenate([latent_a, latent_b], 0).reshape(owners * sub, width)]
    pallas_call x0 -> x2, Pallas kernels: none -> 9.36 us  [the longest x1 5.36 us: fast(): pl.pallas_call(lambda *refs: gated_kernel(*refs, slots=owners, early=earl...]
    another operation x0 -> x5, local copies, waits for them, and re-layouts: none -> 6.07 us
    reduce_sum x3 -> x2, other arithmetic: 5.66 us -> 0.23 us  [the longest x1 0.14 us: fast(): jnp.sum(jnp.where(own_ids[:, :, None] == columns, own_gates[:, :, None],...]
  transfers between devices with their start and end apart: 33 -> 36, of which waited for: 12 -> 14; matrix products, arithmetic and copies ran while one was open for 33% -> 25% of each run, Pallas kernels for 0% -> 2%
where the time goes in v2:
time: 216 us; the launch traced here: 215 us
  waiting for transfers between devices  109 us (50%)
  starting transfers between devices  40.6 us (19%)
  local copies, waits for them, and re-layouts  26.1 us (12%)
  matrix products  24 us (11%)
  Pallas kernels  9.36 us (4%)
  other arithmetic  5.99 us (3%)
    ppermute x3, waiting for transfers between devices, fast(): tables_b.append(lax.ppermute(base_b, 'expert', swaps(owners, k)))  37.7 us
    ppermute x8, waiting for transfers between devices, pair_sum(): got = lax.ppermute(sent, axis, swaps(2, 1))  32.4 us
    dot_general x12, matrix products, dot(): lax.dot_general(lhs, rhs, (dims, ((), ())), preferred_element_type=F32)  24 us
    ppermute x3, waiting for transfers between devices, fast(): far.append(lax.ppermute(half, 'groups', swaps(copies, 1)))  16.5 us
    ppermute x1, waiting for transfers between devices, fast(): forward = lax.ppermute(after(second, first), 'expert', [(1, 0), (2, 3)])  10.7 us
    unnamed x33, local copies, waits for them, and re-layouts  6.68 us
    ppermute x3, starting transfers between devices, fast(): tables_a.append(lax.ppermute(base_a, 'expert', swaps(owners, k)))  6.19 us
    ppermute x8, starting transfers between devices, pair_sum(): got = lax.ppermute(sent, axis, swaps(2, 1))  5.63 us
  transfers between devices with their start and end apart: 36, of which 14 were waited for; matrix products, arithmetic and copies ran while one was open for 25% of the time, Pallas kernels for 2%

profile of v2, /device:TPU:0, one launch (start us, length us, event | category | flops | bytes accessed | tf_op | source)
XLA Modules:
  0.0 214.9 jit_solution(14020438721793457710)
XLA Ops:
  0.0 3.1 %collective-permute-start = (bf16[128,1792]{1,0:T(8,128)(2,1)}, bf16[128,1792]{1,0:T(8,128)(2,1)}, u32[]{:S(2)}, u32[]{:S(2)}) collective-permute-start(bf16[128,1792]{1,0:T(8,128)(2,1)} %param.7), channel_id=1, source_target_pairs={{0,4},{4,0},{8,12},{12,8},{1,5},{5,1},{9,13},{13,9},{2,6},{6,2},{1... | collective-permute-start | bytes 1376264 | tf_op jit(solution)/shard_map/ppermute | solution.py:264
  3.1 2.6 %collective-permute-start.1 = (bf16[128,1792]{1,0:T(8,128)(2,1)}, bf16[128,1792]{1,0:T(8,128)(2,1)}, u32[]{:S(2)}, u32[]{:S(2)}) collective-permute-start(bf16[128,1792]{1,0:T(8,128)(2,1)} %param.7), channel_id=1, source_target_pairs={{0,8},{4,12},{8,0},{12,4},{1,9},{5,13},{9,1},{13,5},{2,10},{6,14},... | collective-permute-start | bytes 1376264 | tf_op jit(solution)/shard_map/ppermute | solution.py:263
  11.9 2.9 %slice.42 = bf16[2,256,1792]{2,1,0:T(8,128)(2,1)} slice(bf16[3,256,1792]{2,1,0:T(8,128)(2,1)} %param.10), slice={[0:2], [0:256], [0:1792]} | slice | bytes 3670016 | tf_op jit(solution)/shard_map/slice | solution.py:287
  14.8 2.6 %fusion.8 = (bf16[1,256,1792]{2,1,0:T(8,128)(2,1)}, bf16[256,1792]{1,0:T(8,128)(2,1)}) fusion(bf16[3,256,1792]{2,1,0:T(8,128)(2,1)} %param.10), kind=kLoop, calls=%fused_computation.66 | loop fusion | bytes 2752512 | tf_op jit(solution)/shard_map/slice | solution.py:307
  18.3 1.9 dynamic-slice_bitcast_fusion
  20.2 3.2 %collective-permute-done = bf16[128,1792]{1,0:T(8,128)(2,1)} collective-permute-done((bf16[128,1792]{1,0:T(8,128)(2,1)}, bf16[128,1792]{1,0:T(8,128)(2,1)}, u32[]{:S(2)}, u32[]{:S(2)}) %collective-permute-start) | collective-permute-done | bytes 458784 | tf_op jit(solution)/shard_map/ppermute | solution.py:264
  25.2 2.0 collective-permute-done.1
  29.0 2.3 %fusion.9 = f32[3,128,512]{2,1,0:T(8,128)S(1)} fusion(bf16[3,128,1792]{2,1,0:T(8,128)(2,1)} %bitcast.121, bf16[512,1792,1]{1,0,2:T(8,128)(2,1)S(1)} %bitcast.100), kind=kOutput, calls=%fused_computation.67 | convolution fusion | flops 704643072 | bytes 3997696 | tf_op jit(solution)/shard_map/dot_general | solution.py:14
  37.3 22.7 %collective-permute-done.3 = bf16[3,32,512]{2,1,0:T(8,128)(2,1)S(1)} collective-permute-done((bf16[3,32,512]{2,1,0:T(8,128)(2,1)S(1)}, bf16[3,32,512]{2,1,0:T(8,128)(2,1)S(1)}, u32[]{:S(2)}, u32[]{:S(2)}) %collective-permute-start.3) | collective-permute-done | bytes 98336 | tf_op jit(solution)/shard_map/ppermute | solution.py:178
  61.5 2.7 %collective-permute-start.4 = (bf16[3,32,512]{2,1,0:T(8,128)(2,1)S(1)}, bf16[3,32,512]{2,1,0:T(8,128)(2,1)}, u32[]{:S(2)}, u32[]{:S(2)}) collective-permute-start(bf16[3,32,512]{2,1,0:T(8,128)(2,1)S(1)} %add_convert_fusion.1.refs_1_), channel_id=1, source_target_pairs={{0,4},{4,0},{8,12},{12,8},{1,5},{5,1},{9,13},{13,9},{2,6},{6,2},{1... | collective-permute-start | bytes 294920 | tf_op jit(solution)/shard_map/ppermute | solution.py:303
  66.1 10.7 %collective-permute-done.8 = bf16[128,1792]{1,0:T(8,128)(2,1)S(1)} collective-permute-done((bf16[128,1792]{1,0:T(8,128)(2,1)}, bf16[128,1792]{1,0:T(8,128)(2,1)S(1)}, u32[]{:S(2)}, u32[]{:S(2)}) %collective-permute-start.8) | collective-permute-done | bytes 458784 | tf_op jit(solution)/shard_map/ppermute | solution.py:283
  81.0 1.9 copy.45
  82.9 1.9 constant_dynamic-slice_fusion.5
  88.9 5.1 %collective-permute-done.15 = bf16[3,32,960]{2,1,0:T(8,128)(2,1)S(1)} collective-permute-done((bf16[3,32,960]{2,1,0:T(8,128)(2,1)}, bf16[3,32,960]{2,1,0:T(8,128)(2,1)S(1)}, u32[]{:S(2)}, u32[]{:S(2)}) %collective-permute-start.15) | collective-permute-done | bytes 184352 | tf_op jit(solution)/shard_map/ppermute | solution.py:178
  101.0 2.8 %collective-permute-done.17 = bf16[1,32,960]{2,1,0:T(8,128)(2,1)S(1)} collective-permute-done((bf16[1,32,960]{2,1,0:T(8,128)(2,1)S(1)}, bf16[1,32,960]{2,1,0:T(8,128)(2,1)S(1)}, u32[]{:S(2)}, u32[]{:S(2)}) %collective-permute-start.17) | collective-permute-done | bytes 61472 | tf_op jit(solution)/shard_map/ppermute | solution.py:178
  103.7 2.5 %collective-permute-start.6 = (bf16[3,32,512]{2,1,0:T(8,128)(2,1)S(1)}, bf16[3,32,512]{2,1,0:T(8,128)(2,1)S(1)}, u32[]{:S(2)}, u32[]{:S(2)}) collective-permute-start(bf16[3,32,512]{2,1,0:T(8,128)(2,1)S(1)} %add_convert_fusion.1.refs_1_), channel_id=1, source_target_pairs={{0,12},{4,8},{8,4},{12,0},{1,13},{5,9},{9,5},{13,1},{2,14},{6,10},... | collective-permute-start | bytes 294920 | tf_op jit(solution)/shard_map/ppermute | solution.py:303
  106.4 2.5 %convolution_convert_fusion.7 = bf16[1024,256]{1,0:T(8,128)(2,1)} fusion(bf16[1024,960]{1,0:T(8,128)(2,1)S(1)} %bitcast.102, bf16[2,960,256]{2,1,0:T(8,128)(2,1)} %param.12), kind=kOutput, calls=%fused_computation.8 | convolution fusion | flops 503578624 | bytes 2981888 | tf_op jit(solution)/shard_map/dot_general | solution.py:14
  108.9 2.6 %convolution_convert_fusion.6 = bf16[1024,256]{1,0:T(8,128)(2,1)} fusion(bf16[1024,960]{1,0:T(8,128)(2,1)S(1)} %bitcast.103, bf16[2,960,256]{2,1,0:T(8,128)(2,1)} %param.12), kind=kOutput, calls=%fused_computation.7 | convolution fusion | flops 503578624 | bytes 2981888 | tf_op jit(solution)/shard_map/dot_general | solution.py:14
  111.6 2.5 %convolution_convert_fusion.5 = bf16[1024,256]{1,0:T(8,128)(2,1)} fusion(bf16[1024,960]{1,0:T(8,128)(2,1)S(1)} %bitcast.104, bf16[2,960,256]{2,1,0:T(8,128)(2,1)} %collective-permute-done.18), kind=kOutput, calls=%fused_computation.6 | convolution fusion | flops 503578624 | bytes 2981888 | tf_op jit(solution)/shard_map/dot_general | solution.py:14
  114.1 2.5 %convolution_convert_fusion.4 = bf16[1024,256]{1,0:T(8,128)(2,1)} fusion(bf16[1024,960]{1,0:T(8,128)(2,1)S(1)} %bitcast.105, bf16[2,960,256]{2,1,0:T(8,128)(2,1)} %collective-permute-done.18), kind=kOutput, calls=%fused_computation.5 | convolution fusion | flops 503578624 | bytes 2981888 | tf_op jit(solution)/shard_map/dot_general | solution.py:14
  116.7 2.5 %convolution_convert_fusion.3 = bf16[1024,256]{1,0:T(8,128)(2,1)} fusion(bf16[1024,960]{1,0:T(8,128)(2,1)S(1)} %bitcast.106, bf16[2,960,256]{2,1,0:T(8,128)(2,1)} %collective-permute-done.19), kind=kOutput, calls=%fused_computation.4 | convolution fusion | flops 503578624 | bytes 2981888 | tf_op jit(solution)/shard_map/dot_general | solution.py:14
  119.2 2.6 %convolution_convert_fusion.2 = bf16[1024,256]{1,0:T(8,128)(2,1)} fusion(bf16[1024,960]{1,0:T(8,128)(2,1)S(1)} %bitcast.107, bf16[2,960,256]{2,1,0:T(8,128)(2,1)} %collective-permute-done.19), kind=kOutput, calls=%fused_computation.3 | convolution fusion | flops 503578624 | bytes 2981888 | tf_op jit(solution)/shard_map/dot_general | solution.py:14
  121.8 1.9 collective-permute-start.11
  125.2 2.4 %collective-permute-start.32 = (bf16[128,1792]{1,0:T(8,128)(2,1)}, bf16[128,1792]{1,0:T(8,128)(2,1)}, u32[]{:S(2)}, u32[]{:S(2)}) collective-permute-start(bf16[128,1792]{1,0:T(8,128)(2,1)} %dynamic-slice_bitcast_fusion), channel_id=1, source_target_pairs={{0,12},{4,8},{8,4},{12,0},{1,13},{5,9},{9,5},{13,1},{2,14},{6,10},... | collective-permute-start | bytes 1376264 | tf_op jit(solution)/shard_map/ppermute | solution.py:312
  128.6 2.5 %collective-permute-start.13 = (bf16[1,32,512]{2,1,0:T(8,128)(2,1)S(1)}, bf16[1,32,512]{2,1,0:T(8,128)(2,1)S(1)}, u32[]{:S(2)}, u32[]{:S(2)}) collective-permute-start(bf16[1,32,512]{2,1,0:T(8,128)(2,1)S(1)} %add_convert_fusion.3.refs_5_), channel_id=1, source_target_pairs={{0,12},{4,8},{8,4},{12,0},{1,13},{5,9},{9,5},{13,1},{2,14},{6,10},... | collective-permute-start | bytes 98312 | tf_op jit(solution)/shard_map/ppermute | solution.py:305
  132.6 37.7 %collective-permute-done.12.refs_7_ = bf16[1,32,512]{2,1,0:T(8,128)(2,1)S(1)} collective-permute-done((bf16[1,32,512]{2,1,0:T(8,128)(2,1)S(1)}, bf16[1,32,512]{2,1,0:T(8,128)(2,1)S(1)}, u32[]{:S(2)}, u32[]{:S(2)}) %collective-permute-start.12) | collective-permute-done | bytes 32800 | tf_op jit(solution)/shard_map/ppermute | solution.py:305
  171.0 5.4 %gated.1 = bf16[4,8,32,128]{3,2,1,0:T(8,128)(2,1)} custom-call(s32[2]{0:T(128)} %pad_add_fusion.refs_0_, bf16[3,32,512]{2,1,0:T(8,128)(2,1)} %copy-done.6, bf16[3,32,512]{2,1,0:T(8,128)(2,1)} %collective-permute-done.4.refs_2_, bf16[3,32,512]{2,1,0:T(8,128)(2,1)} %collective-permute-done.5.refs_3_, bf16[3,32,512]{2,1,0:T(8,128)(2,1)} %copy-done.10, ...), custom_call_target="tpu_custom_call" | custom-call | tf_op jit(solution)/shard_map/gated/pallas_call | solution.py:332
  185.3 2.8 %collective-permute-done.25 = bf16[8,32,128]{2,1,0:T(8,128)(2,1)S(1)} collective-permute-done((bf16[8,32,128]{2,1,0:T(8,128)(2,1)S(1)}, bf16[8,32,128]{2,1,0:T(8,128)(2,1)S(1)}, u32[]{:S(2)}, u32[]{:S(2)}) %collective-permute-start.25) | collective-permute-done | bytes 65568 | tf_op jit(solution)/shard_map/ppermute | solution.py:344
  190.9 2.9 %collective-permute-done.27.refs_2_ = bf16[8,32,128]{2,1,0:T(8,128)(2,1)} collective-permute-done((bf16[8,32,128]{2,1,0:T(8,128)(2,1)S(1)}, bf16[8,32,128]{2,1,0:T(8,128)(2,1)}, u32[]{:S(2)}, u32[]{:S(2)}) %collective-permute-start.27) | collective-permute-done | bytes 65568 | tf_op jit(solution)/shard_map/ppermute | solution.py:346
  194.4 7.9 %collective-permute-done.34.refs_10_ = bf16[128,1792]{1,0:T(8,128)(2,1)} collective-permute-done((bf16[128,1792]{1,0:T(8,128)(2,1)}, bf16[128,1792]{1,0:T(8,128)(2,1)}, u32[]{:S(2)}, u32[]{:S(2)}) %collective-permute-start.34) | collective-permute-done | bytes 458784 | tf_op jit(solution)/shard_map/ppermute | solution.py:314
  202.3 8.6 %collective-permute-done.35.refs_11_ = bf16[128,1792]{1,0:T(8,128)(2,1)} collective-permute-done((bf16[128,1792]{1,0:T(8,128)(2,1)}, bf16[128,1792]{1,0:T(8,128)(2,1)}, u32[]{:S(2)}, u32[]{:S(2)}) %collective-permute-start.35) | collective-permute-done | bytes 458784 | tf_op jit(solution)/shard_map/ppermute | solution.py:314
  210.9 4.0 %final.1 = bf16[128,1792]{1,0:T(8,128)(2,1)} custom-call(s32[12]{0:T(128)} %stack.75.refs_0_, bf16[8,32,128]{2,1,0:T(8,128)(2,1)} %copy-done.7, bf16[8,32,128]{2,1,0:T(8,128)(2,1)} %collective-permute-done.27.refs_2_, bf16[8,32,128]{2,1,0:T(8,128)(2,1)} %collective-permute-done.28.refs_3_, bf16[8,32,128]{2,1,0:T(8,128)(2,1)} %collective-permute-done.29.refs_4_, ...), custom_call_target="tpu_custom_call" | custom-call | tf_op jit(solution)/shard_map/final/pallas_call | solution.py:364
  (126 shorter events, 52.5 us)
Async XLA Ops:
  0.0 23.4 %collective-permute-start = (bf16[128,1792]{1,0:T(8,128)(2,1)}, bf16[128,1792]{1,0:T(8,128)(2,1)}, u32[]{:S(2)}, u32[]{:S(2)}) collective-permute-start(bf16[128,1792]{1,0:T(8,128)(2,1)} %param.7), channel_id=1, source_target_pairs={{0,4},{4,0},{8,12},{12,8},{1,5},{5,1},{9,13},{13,9},{2,6},{6,2},{1... | collective-permute-start | bytes 1376264 | tf_op jit(solution)/shard_map/ppermute | solution.py:264
  3.1 24.2 %collective-permute-start.1 = (bf16[128,1792]{1,0:T(8,128)(2,1)}, bf16[128,1792]{1,0:T(8,128)(2,1)}, u32[]{:S(2)}, u32[]{:S(2)}) collective-permute-start(bf16[128,1792]{1,0:T(8,128)(2,1)} %param.7), channel_id=1, source_target_pairs={{0,8},{4,12},{8,0},{12,4},{1,9},{5,13},{9,1},{13,5},{2,10},{6,14},... | collective-permute-start | bytes 1376264 | tf_op jit(solution)/shard_map/ppermute | solution.py:263
  5.6 105.8 %collective-permute-start.18 = (bf16[2,960,256]{2,1,0:T(8,128)(2,1)}, bf16[2,960,256]{2,1,0:T(8,128)(2,1)}, u32[]{:S(2)}, u32[]{:S(2)}) collective-permute-start(bf16[2,960,256]{2,1,0:T(8,128)(2,1)} %param.12), channel_id=1, source_target_pairs={{0,1},{1,0},{2,3},{3,2},{4,5},{5,4},{6,7},{7,6},{8,9},{9,8},{10,11... | collective-permute-start | bytes 2949128 | tf_op jit(solution)/shard_map/ppermute | solution.py:278
  8.2 25.7 %collective-permute-start.23 = (f32[32,8]{1,0:T(8,128)}, f32[32,8]{1,0:T(8,128)S(1)}, u32[]{:S(2)}, u32[]{:S(2)}) collective-permute-start(f32[32,8]{1,0:T(8,128)} %get-tuple-element.17), channel_id=1, source_target_pairs={{0,12},{4,8},{8,4},{12,0},{1,13},{5,9},{9,5},{13,1},{2,14},{6,10},... | collective-permute-start | bytes 3080 | tf_op jit(solution)/shard_map/ppermute | solution.py:272
  8.3 27.1 %collective-permute-start.22 = (f32[32,8]{1,0:T(8,128)S(1)}, f32[32,8]{1,0:T(8,128)S(1)}, u32[]{:S(2)}, u32[]{:S(2)}) collective-permute-start(f32[32,8]{1,0:T(8,128)S(1)} %get-tuple-element.18), channel_id=1, source_target_pairs={{0,8},{4,12},{8,0},{12,4},{1,9},{5,13},{9,1},{13,5},{2,10},{6,14},... | collective-permute-start | bytes 3080 | tf_op jit(solution)/shard_map/ppermute | solution.py:272
  23.4 12.6 %collective-permute-start.21 = (f32[32,8]{1,0:T(8,128)S(1)}, f32[32,8]{1,0:T(8,128)S(1)}, u32[]{:S(2)}, u32[]{:S(2)}) collective-permute-start(f32[32,8]{1,0:T(8,128)S(1)} %get-tuple-element.19), channel_id=1, source_target_pairs={{0,4},{4,0},{8,12},{12,8},{1,5},{5,1},{9,13},{13,9},{2,6},{6,2},{1... | collective-permute-start | bytes 3080 | tf_op jit(solution)/shard_map/ppermute | solution.py:272
  33.2 28.2 %collective-permute-start.14 = (bf16[3,64,960]{2,1,0:T(8,128)(2,1)S(1)}, bf16[3,64,960]{2,1,0:T(8,128)(2,1)S(1)}, u32[]{:S(2)}, u32[]{:S(2)}) collective-permute-start(bf16[3,64,960]{2,1,0:T(8,128)(2,1)S(1)} %dynamic-slice_convert_fusion), channel_id=1, source_target_pairs={{0,1},{1,0},{2,3},{3,2},{4,5},{5,4},{6,7},{7,6},{8,9},{9,8},{10,11... | collective-permute-start | bytes 1105928 | tf_op jit(solution)/shard_map/ppermute | solution.py:178
  33.9 77.6 %collective-permute-start.19 = (bf16[2,960,256]{2,1,0:T(8,128)(2,1)}, bf16[2,960,256]{2,1,0:T(8,128)(2,1)}, u32[]{:S(2)}, u32[]{:S(2)}) collective-permute-start(bf16[2,960,256]{2,1,0:T(8,128)(2,1)} %param.12), channel_id=1, source_target_pairs={{0,2},{2,0},{1,3},{3,1},{4,6},{6,4},{5,7},{7,5},{8,10},{10,8},{9,1... | collective-permute-start | bytes 2949128 | tf_op jit(solution)/shard_map/ppermute | solution.py:275
  35.4 24.5 %collective-permute-start.3 = (bf16[3,32,512]{2,1,0:T(8,128)(2,1)S(1)}, bf16[3,32,512]{2,1,0:T(8,128)(2,1)S(1)}, u32[]{:S(2)}, u32[]{:S(2)}) collective-permute-start(bf16[3,32,512]{2,1,0:T(8,128)(2,1)S(1)} %dynamic-slice_convert_fusion.3), channel_id=1, source_target_pairs={{0,2},{2,0},{1,3},{3,1},{4,6},{6,4},{5,7},{7,5},{8,10},{10,8},{9,1... | collective-permute-start | bytes 294920 | tf_op jit(solution)/shard_map/ppermute | solution.py:178
  36.6 28.5 %collective-permute-start.7 = (bf16[128,1792]{1,0:T(8,128)(2,1)S(1)}, bf16[128,1792]{1,0:T(8,128)(2,1)S(1)}, u32[]{:S(2)}, u32[]{:S(2)}) collective-permute-start(bf16[128,1792]{1,0:T(8,128)(2,1)S(1)} %copy-done.5), channel_id=1, source_target_pairs={{4,8},{8,4},{5,9},{9,5},{6,10},{10,6},{7,11},{11,7},{20,24},{24,20... | collective-permute-start | bytes 1376264 | tf_op jit(solution)/shard_map/ppermute | solution.py:284
  59.9 16.9 %collective-permute-start.8 = (bf16[128,1792]{1,0:T(8,128)(2,1)}, bf16[128,1792]{1,0:T(8,128)(2,1)S(1)}, u32[]{:S(2)}, u32[]{:S(2)}) collective-permute-start(bf16[128,1792]{1,0:T(8,128)(2,1)} %collective-permute-done.1), channel_id=1, source_target_pairs={{4,0},{8,12},{5,1},{9,13},{6,2},{10,14},{7,3},{11,15},{20,16},{24,... | collective-permute-start | bytes 1376264 | tf_op jit(solution)/shard_map/ppermute | solution.py:283
  61.5 63.7 %collective-permute-start.4 = (bf16[3,32,512]{2,1,0:T(8,128)(2,1)S(1)}, bf16[3,32,512]{2,1,0:T(8,128)(2,1)}, u32[]{:S(2)}, u32[]{:S(2)}) collective-permute-start(bf16[3,32,512]{2,1,0:T(8,128)(2,1)S(1)} %add_convert_fusion.1.refs_1_), channel_id=1, source_target_pairs={{0,4},{4,0},{8,12},{12,8},{1,5},{5,1},{9,13},{13,9},{2,6},{6,2},{1... | collective-permute-start | bytes 294920 | tf_op jit(solution)/shard_map/ppermute | solution.py:303
  65.1 60.1 %collective-permute-start.5 = (bf16[3,32,512]{2,1,0:T(8,128)(2,1)S(1)}, bf16[3,32,512]{2,1,0:T(8,128)(2,1)}, u32[]{:S(2)}, u32[]{:S(2)}) collective-permute-start(bf16[3,32,512]{2,1,0:T(8,128)(2,1)S(1)} %add_convert_fusion.1.refs_1_), channel_id=1, source_target_pairs={{0,8},{4,12},{8,0},{12,4},{1,9},{5,13},{9,1},{13,5},{2,10},{6,14},... | collective-permute-start | bytes 294920 | tf_op jit(solution)/shard_map/ppermute | solution.py:303
  80.0 6.5 %collective-permute-start.9 = (bf16[1,64,512]{2,1,0:T(8,128)(2,1)}, bf16[1,64,512]{2,1,0:T(8,128)(2,1)}, u32[]{:S(2)}, u32[]{:S(2)}) collective-permute-start(bf16[1,64,512]{2,1,0:T(8,128)(2,1)} %fusion.7), channel_id=1, source_target_pairs={{0,1},{1,0},{2,3},{3,2},{4,5},{5,4},{6,7},{7,6},{8,9},{9,8},{10,11... | collective-permute-start | bytes 196616 | tf_op jit(solution)/shard_map/ppermute | solution.py:178
  86.4 7.5 %collective-permute-start.15 = (bf16[3,32,960]{2,1,0:T(8,128)(2,1)}, bf16[3,32,960]{2,1,0:T(8,128)(2,1)S(1)}, u32[]{:S(2)}, u32[]{:S(2)}) collective-permute-start(bf16[3,32,960]{2,1,0:T(8,128)(2,1)} %dynamic-slice_convert_fusion.1), channel_id=1, source_target_pairs={{0,2},{2,0},{1,3},{3,1},{4,6},{6,4},{5,7},{7,5},{8,10},{10,8},{9,1... | collective-permute-start | bytes 552968 | tf_op jit(solution)/shard_map/ppermute | solution.py:178
  103.7 23.9 %collective-permute-start.6 = (bf16[3,32,512]{2,1,0:T(8,128)(2,1)S(1)}, bf16[3,32,512]{2,1,0:T(8,128)(2,1)S(1)}, u32[]{:S(2)}, u32[]{:S(2)}) collective-permute-start(bf16[3,32,512]{2,1,0:T(8,128)(2,1)S(1)} %add_convert_fusion.1.refs_1_), channel_id=1, source_target_pairs={{0,12},{4,8},{8,4},{12,0},{1,13},{5,9},{9,5},{13,1},{2,14},{6,10},... | collective-permute-start | bytes 294920 | tf_op jit(solution)/shard_map/ppermute | solution.py:303
  111.5 67.3 %collective-permute-start.30 = (bf16[128,1792]{1,0:T(8,128)(2,1)}, bf16[128,1792]{1,0:T(8,128)(2,1)}, u32[]{:S(2)}, u32[]{:S(2)}) collective-permute-start(bf16[128,1792]{1,0:T(8,128)(2,1)} %dynamic-slice_bitcast_fusion), channel_id=1, source_target_pairs={{0,4},{4,0},{8,12},{12,8},{1,5},{5,1},{9,13},{13,9},{2,6},{6,2},{1... | collective-permute-start | bytes 1376264 | tf_op jit(solution)/shard_map/ppermute | solution.py:312
  111.5 10.3 %collective-permute-start.20 = (bf16[2,960,256]{2,1,0:T(8,128)(2,1)}, bf16[2,960,256]{2,1,0:T(8,128)(2,1)S(1)}, u32[]{:S(2)}, u32[]{:S(2)}) collective-permute-start(bf16[2,960,256]{2,1,0:T(8,128)(2,1)} %collective-permute-done.19), channel_id=1, source_target_pairs={{0,1},{1,0},{2,3},{3,2},{4,5},{5,4},{6,7},{7,6},{8,9},{9,8},{10,11... | collective-permute-start | bytes 2949128 | tf_op jit(solution)/shard_map/ppermute | solution.py:280
  121.8 6.9 %collective-permute-start.11 = (bf16[1,32,512]{2,1,0:T(8,128)(2,1)S(1)}, bf16[1,32,512]{2,1,0:T(8,128)(2,1)S(1)}, u32[]{:S(2)}, u32[]{:S(2)}) collective-permute-start(bf16[1,32,512]{2,1,0:T(8,128)(2,1)S(1)} %add_convert_fusion.3.refs_5_), channel_id=1, source_target_pairs={{0,4},{4,0},{8,12},{12,8},{1,5},{5,1},{9,13},{13,9},{2,6},{6,2},{1... | collective-permute-start | bytes 98312 | tf_op jit(solution)/shard_map/ppermute | solution.py:305
  125.2 55.1 %collective-permute-start.31 = (bf16[128,1792]{1,0:T(8,128)(2,1)}, bf16[128,1792]{1,0:T(8,128)(2,1)}, u32[]{:S(2)}, u32[]{:S(2)}) collective-permute-start(bf16[128,1792]{1,0:T(8,128)(2,1)} %dynamic-slice_bitcast_fusion), channel_id=1, source_target_pairs={{0,8},{4,12},{8,0},{12,4},{1,9},{5,13},{9,1},{13,5},{2,10},{6,14},... | collective-permute-start | bytes 1376264 | tf_op jit(solution)/shard_map/ppermute | solution.py:312
  125.2 55.6 %collective-permute-start.32 = (bf16[128,1792]{1,0:T(8,128)(2,1)}, bf16[128,1792]{1,0:T(8,128)(2,1)}, u32[]{:S(2)}, u32[]{:S(2)}) collective-permute-start(bf16[128,1792]{1,0:T(8,128)(2,1)} %dynamic-slice_bitcast_fusion), channel_id=1, source_target_pairs={{0,12},{4,8},{8,4},{12,0},{1,13},{5,9},{9,5},{13,1},{2,14},{6,10},... | collective-permute-start | bytes 1376264 | tf_op jit(solution)/shard_map/ppermute | solution.py:312
  127.7 42.7 %collective-permute-start.12 = (bf16[1,32,512]{2,1,0:T(8,128)(2,1)S(1)}, bf16[1,32,512]{2,1,0:T(8,128)(2,1)S(1)}, u32[]{:S(2)}, u32[]{:S(2)}) collective-permute-start(bf16[1,32,512]{2,1,0:T(8,128)(2,1)S(1)} %add_convert_fusion.3.refs_5_), channel_id=1, source_target_pairs={{0,8},{4,12},{8,0},{12,4},{1,9},{5,13},{9,1},{13,5},{2,10},{6,14},... | collective-permute-start | bytes 98312 | tf_op jit(solution)/shard_map/ppermute | solution.py:305
  128.6 41.7 %collective-permute-start.13 = (bf16[1,32,512]{2,1,0:T(8,128)(2,1)S(1)}, bf16[1,32,512]{2,1,0:T(8,128)(2,1)S(1)}, u32[]{:S(2)}, u32[]{:S(2)}) collective-permute-start(bf16[1,32,512]{2,1,0:T(8,128)(2,1)S(1)} %add_convert_fusion.3.refs_5_), channel_id=1, source_target_pairs={{0,12},{4,8},{8,4},{12,0},{1,13},{5,9},{9,5},{13,1},{2,14},{6,10},... | collective-permute-start | bytes 98312 | tf_op jit(solution)/shard_map/ppermute | solution.py:305
  177.2 6.3 %collective-permute-start.26 = (bf16[8,32,128]{2,1,0:T(8,128)(2,1)S(1)}, bf16[8,32,128]{2,1,0:T(8,128)(2,1)S(1)}, u32[]{:S(2)}, u32[]{:S(2)}) collective-permute-start(bf16[8,32,128]{2,1,0:T(8,128)(2,1)S(1)} %get-tuple-element.14), channel_id=1, source_target_pairs={{0,12},{4,8},{8,4},{12,0},{1,13},{5,9},{9,5},{13,1},{2,14},{6,10},... | collective-permute-start | bytes 196616 | tf_op jit(solution)/shard_map/ppermute | solution.py:344
  178.8 15.6 %collective-permute-start.33 = (bf16[128,1792]{1,0:T(8,128)(2,1)}, bf16[128,1792]{1,0:T(8,128)(2,1)}, u32[]{:S(2)}, u32[]{:S(2)}) collective-permute-start(bf16[128,1792]{1,0:T(8,128)(2,1)} %collective-permute-done.30.refs_6_), channel_id=1, source_target_pairs={{0,16},{16,0},{1,17},{17,1},{2,18},{18,2},{3,19},{19,3},{4,20},{20... | collective-permute-start | bytes 1376264 | tf_op jit(solution)/shard_map/ppermute | solution.py:314
  180.3 22.0 %collective-permute-start.34 = (bf16[128,1792]{1,0:T(8,128)(2,1)}, bf16[128,1792]{1,0:T(8,128)(2,1)}, u32[]{:S(2)}, u32[]{:S(2)}) collective-permute-start(bf16[128,1792]{1,0:T(8,128)(2,1)} %collective-permute-done.31.refs_7_), channel_id=1, source_target_pairs={{0,16},{16,0},{1,17},{17,1},{2,18},{18,2},{3,19},{19,3},{4,20},{20... | collective-permute-start | bytes 1376264 | tf_op jit(solution)/shard_map/ppermute | solution.py:314
  180.8 30.1 %collective-permute-start.35 = (bf16[128,1792]{1,0:T(8,128)(2,1)}, bf16[128,1792]{1,0:T(8,128)(2,1)}, u32[]{:S(2)}, u32[]{:S(2)}) collective-permute-start(bf16[128,1792]{1,0:T(8,128)(2,1)} %collective-permute-done.32.refs_8_), channel_id=1, source_target_pairs={{0,16},{16,0},{1,17},{17,1},{2,18},{18,2},{3,19},{19,3},{4,20},{20... | collective-permute-start | bytes 1376264 | tf_op jit(solution)/shard_map/ppermute | solution.py:314
  182.3 5.7 %collective-permute-start.25 = (bf16[8,32,128]{2,1,0:T(8,128)(2,1)S(1)}, bf16[8,32,128]{2,1,0:T(8,128)(2,1)S(1)}, u32[]{:S(2)}, u32[]{:S(2)}) collective-permute-start(bf16[8,32,128]{2,1,0:T(8,128)(2,1)S(1)} %get-tuple-element.15), channel_id=1, source_target_pairs={{0,8},{4,12},{8,0},{12,4},{1,9},{5,13},{9,1},{13,5},{2,10},{6,14},... | collective-permute-start | bytes 196616 | tf_op jit(solution)/shard_map/ppermute | solution.py:344
  183.5 4.9 %collective-permute-start.24 = (bf16[8,32,128]{2,1,0:T(8,128)(2,1)S(1)}, bf16[8,32,128]{2,1,0:T(8,128)(2,1)S(1)}, u32[]{:S(2)}, u32[]{:S(2)}) collective-permute-start(bf16[8,32,128]{2,1,0:T(8,128)(2,1)S(1)} %get-tuple-element.13), channel_id=1, source_target_pairs={{0,4},{4,0},{8,12},{12,8},{1,5},{5,1},{9,13},{13,9},{2,6},{6,2},{1... | collective-permute-start | bytes 196616 | tf_op jit(solution)/shard_map/ppermute | solution.py:344
  189.4 4.4 %collective-permute-start.27 = (bf16[8,32,128]{2,1,0:T(8,128)(2,1)S(1)}, bf16[8,32,128]{2,1,0:T(8,128)(2,1)}, u32[]{:S(2)}, u32[]{:S(2)}) collective-permute-start(bf16[8,32,128]{2,1,0:T(8,128)(2,1)S(1)} %fusion.6.refs_1_), channel_id=1, source_target_pairs={{0,2},{2,0},{1,3},{3,1},{4,6},{6,4},{5,7},{7,5},{8,10},{10,8},{9,1... | collective-permute-start | bytes 196616 | tf_op jit(solution)/shard_map/ppermute | solution.py:346
  190.9 20.0 %collective-permute-start.28 = (bf16[8,32,128]{2,1,0:T(8,128)(2,1)S(1)}, bf16[8,32,128]{2,1,0:T(8,128)(2,1)}, u32[]{:S(2)}, u32[]{:S(2)}) collective-permute-start(bf16[8,32,128]{2,1,0:T(8,128)(2,1)S(1)} %fusion.6.refs_1_), channel_id=1, source_target_pairs={{0,1},{1,0},{2,3},{3,2},{4,5},{5,4},{6,7},{7,6},{8,9},{9,8},{10,11... | collective-permute-start | bytes 196616 | tf_op jit(solution)/shard_map/ppermute | solution.py:347
  193.8 17.1 %collective-permute-start.29 = (bf16[8,32,128]{2,1,0:T(8,128)(2,1)}, bf16[8,32,128]{2,1,0:T(8,128)(2,1)}, u32[]{:S(2)}, u32[]{:S(2)}) collective-permute-start(bf16[8,32,128]{2,1,0:T(8,128)(2,1)} %collective-permute-done.27.refs_2_), channel_id=1, source_target_pairs={{0,1},{1,0},{2,3},{3,2},{4,5},{5,4},{6,7},{7,6},{8,9},{9,8},{10,11... | collective-permute-start | bytes 196616 | tf_op jit(solution)/shard_map/ppermute | solution.py:347
  (19 other events, 254.7 us)
